TPU v7x, 512 devices: a whole 4x8x8 slice. The times are simulated.
512 devices in a mesh: lag: 8 (over y), patch: 64 (over z, x, core).
Axes of the slice: x: 4, y: 8, z: 8, core: 2. Of those that a mesh axis runs over, the one named last changes fastest.
Arguments:
- incident: bfloat16 [4, 32768, 128], P(None, 'patch'), may hold values from -6 to 6
- pending: float32 [8, 32768, 128], P('lag', 'patch'), may hold values from -6 to 6
- self_inverse: float32 [256, 128, 128], P('patch'), may hold values from -0.5 to 0.5
- retarded: float32 [8, 64, 56, 128, 128], P('lag', 'patch'), may hold values from -0.1875 to 0.1875
- block_rows: int32 [8, 64, 56], P('lag', 'patch'), may hold values from -1 to 3, as said below
- block_sources: int32 [8, 64, 56], P('lag', 'patch'), may hold values from -1 to 255, as said below
- owner_map: int32 [256], replicated, may hold values from 0 to 255, as said below
Outputs:
- currents: bfloat16 [4, 32768, 128], P(None, 'patch')
- fields_ahead: float32 [8, 32768, 128], P('lag', 'patch')
Inputs may be any that keep to these rules, and one draw needn't show every extreme that they name: `block_sources`: each device's list holds its live entries first and -1 after them; at most 56 live entries, a count that some device reaches in every draw; the live entries of one device name no (row, source) pair twice and, among them, at most one storage block of each patch owner. `block_rows`: -1 exactly where block_sources is -1. `owner_map`: A permutation of the 256 storage blocks; storage block q is owned by patch q // 4.
All inputs are finite; a program needn't handle non-finite values.
Results may differ from a plain program's by a relative error of at most 0.0055.
Values may be sent and summed in bfloat16 or wider, within the bound.
A program may use at most 64 MiB of HBM per device.

v0:
```python
import jax
import jax.numpy as jnp
from jax import lax
from jax.sharding import PartitionSpec as P

EXC = 128
BSIZE = 128
BLK_DEV = 4
STEPS = 4


def broadcast(x, axis, root):
    mine = lax.axis_index(axis) == root
    return lax.psum(jnp.where(mine, x, jnp.zeros_like(x)), axis)


def shifted(x, axis, by):
    size = lax.axis_size(axis)
    pairs = [(i, i + by) for i in range(size) if 0 <= i + by < size]
    return lax.ppermute(x, axis, pairs)


def solve_blocks(excess, self_inverse):
    blocks = excess.reshape(BLK_DEV, BSIZE, EXC)
    solved = jnp.einsum("kab,kbe->kae", self_inverse, blocks, precision=lax.Precision.HIGHEST)
    return solved.reshape(BLK_DEV * BSIZE, EXC).astype(jnp.bfloat16)


def lag_part(current, asked_local, owner_patch, weights, row_select):
    blocks = current.reshape(BLK_DEV, BSIZE, EXC)
    chosen = blocks[jnp.maximum(asked_local, 0)]
    outgoing = jnp.where((asked_local >= 0)[:, None, None], chosen, jnp.zeros_like(chosen))
    arrived = lax.all_to_all(outgoing, "patch", split_axis=0, concat_axis=0, tiled=True)
    picked = arrived[owner_patch].astype(jnp.float32)
    product = jnp.einsum("jab,jbe->jae", weights, picked, precision=lax.Precision.HIGHEST)
    summed = jnp.einsum("jr,jae->rae", row_select, product, precision=lax.Precision.HIGHEST)
    return summed.reshape(BLK_DEV * BSIZE, EXC)


def body(incident, pending, self_inverse, retarded, block_rows, block_sources, owner_map):
    patches = lax.axis_size("patch")
    weights = retarded[0, 0]
    row_index = block_rows[0, 0]
    source_index = block_sources[0, 0]
    is_live = source_index >= 0
    storage = owner_map[jnp.maximum(source_index, 0)]
    owner_patch = storage // BLK_DEV
    local_block = storage % BLK_DEV
    matches = (owner_patch[:, None] == jnp.arange(patches)[None, :]) & is_live[:, None]
    wanted = jnp.max(jnp.where(matches, local_block[:, None], -1), axis=0)
    asked_local = lax.all_to_all(
        wanted.reshape(patches, 1), "patch", split_axis=0, concat_axis=0, tiled=True
    ).reshape(patches)
    row_select = (row_index[:, None] == jnp.arange(BLK_DEV)[None, :]).astype(jnp.float32)
    currents = []
    partial_field = pending[0]
    for time_step in range(STEPS):
        current = solve_blocks(
            incident[time_step].astype(jnp.float32) - partial_field, self_inverse
        )
        current = broadcast(current, "lag", 0)
        currents.append(current)
        fresh = lag_part(current, asked_local, owner_patch, weights, row_select)
        partial_field = shifted(partial_field, "lag", -1) + fresh
    fields_ahead = partial_field[None]
    return (jnp.stack(currents), fields_ahead)


def solution(mesh):
    in_specs = (
        P(None, "patch", None),
        P("lag", "patch", None),
        P("patch", None, None),
        P("lag", "patch", None, None, None),
        P("lag", "patch", None),
        P("lag", "patch", None),
        P(),
    )
    out_specs = (P(None, "patch", None), P("lag", "patch", None))
    return jax.shard_map(body, mesh=mesh, in_specs=in_specs, out_specs=out_specs, check_vma=False)
```

profile of v0, /device:TPU:2, one launch (start us, length us, event | category | flops | bytes accessed | tf_op | source)
XLA Modules:
  0.0 667.6 jit_solution(8748012955424991458)
XLA Ops:
  10.9 13.9 %all-to-all-start = ((s32[64,1,1]{2,1,0:T(1,128)}), s32[64,1,1]{2,1,0:T(1,128)S(1)}, u32[]{:S(2)}, u32[]{:S(2)}) async-start(s32[64,1,1]{2,1,0:T(1,128)} %copy.35), calls=%async_computation | async-start | bytes 65536 | tf_op jit(solution)/shard_map/all_to_all | solution.py:51
  26.9 6.4 all-to-all-done
  35.8 71.5 %all-reduce.5.cloned.1.call-done = bf16[512,128]{1,0:T(8,128)(2,1)} async-done(((bf16[512,128]{1,0:T(8,128)(2,1)}), bf16[512,128]{1,0:T(8,128)(2,1)}) %all-reduce.5.cloned.1.call-update) | async-done | bytes 131088 | tf_op jit(solution)/shard_map/psum | solution.py:14
  107.2 1.9 gather_fusion.1
  110.7 11.0 %all-to-all-start.1 = ((bf16[64,128,128]{2,1,0:T(8,128)(2,1)}), bf16[64,128,128]{2,1,0:T(8,128)(2,1)S(1)}, u32[]{:S(2)}, u32[]{:S(2)}) async-start(bf16[64,128,128]{2,1,0:T(8,128)(2,1)} %broadcast_select_fusion.3), calls=%async_computation.1 | async-start | bytes 4194304 | tf_op jit(solution)/shard_map/all_to_all | solution.py:33
  123.1 49.8 %all-to-all-done.1 = bf16[64,128,128]{2,1,0:T(8,128)(2,1)S(1)} async-done(((bf16[64,128,128]{2,1,0:T(8,128)(2,1)}), bf16[64,128,128]{2,1,0:T(8,128)(2,1)S(1)}, u32[]{:S(2)}, u32[]{:S(2)}) %all-to-all-start.1) | async-done | bytes 2097184 | tf_op jit(solution)/shard_map/all_to_all | solution.py:33
  172.9 2.1 gather_fusion.2
  175.0 8.1 %fusion.8 = f32[56,128,128]{1,2,0:T(8,128)} fusion(bf16[56,128,128]{2,1,0:T(8,128)(2,1)} %gather_fusion.2, f32[1,1,56,128,128]{4,3,2,1,0:T(8,128)} %param.10), kind=kOutput, calls=%fused_computation.21 | convolution fusion | flops 1409286144 | bytes 9175040 | tf_op jit(solution)/shard_map/jab,jbe->jae/dot_general | solution.py:35
  183.2 4.6 copy.37
  187.8 3.4 fusion.33
  192.3 71.2 %all-reduce.7.cloned.1.call-done = bf16[512,128]{1,0:T(8,128)(2,1)} async-done(((bf16[512,128]{1,0:T(8,128)(2,1)}), bf16[512,128]{1,0:T(8,128)(2,1)}) %all-reduce.7.cloned.1.call-update) | async-done | bytes 131088 | tf_op jit(solution)/shard_map/psum | solution.py:14
  263.5 1.9 gather_fusion.3
  266.9 10.9 %all-to-all-start.2 = ((bf16[64,128,128]{2,1,0:T(8,128)(2,1)}), bf16[64,128,128]{2,1,0:T(8,128)(2,1)S(1)}, u32[]{:S(2)}, u32[]{:S(2)}) async-start(bf16[64,128,128]{2,1,0:T(8,128)(2,1)} %broadcast_select_fusion.2), calls=%async_computation.2 | async-start | bytes 4194304 | tf_op jit(solution)/shard_map/all_to_all | solution.py:33
  279.1 49.9 %all-to-all-done.2 = bf16[64,128,128]{2,1,0:T(8,128)(2,1)S(1)} async-done(((bf16[64,128,128]{2,1,0:T(8,128)(2,1)}), bf16[64,128,128]{2,1,0:T(8,128)(2,1)S(1)}, u32[]{:S(2)}, u32[]{:S(2)}) %all-to-all-start.2) | async-done | bytes 2097184 | tf_op jit(solution)/shard_map/all_to_all | solution.py:33
  329.0 2.1 gather_fusion.4
  331.1 8.1 %fusion.11 = f32[56,128,128]{1,2,0:T(8,128)} fusion(bf16[56,128,128]{2,1,0:T(8,128)(2,1)} %gather_fusion.4, f32[1,1,56,128,128]{4,3,2,1,0:T(8,128)} %param.10), kind=kOutput, calls=%fused_computation.22 | convolution fusion | flops 1409286144 | bytes 9175040 | tf_op jit(solution)/shard_map/jab,jbe->jae/dot_general | solution.py:35
  339.2 4.6 copy.40
  343.8 3.3 fusion.31
  348.3 71.2 %all-reduce.9.cloned.1.call-done = bf16[512,128]{1,0:T(8,128)(2,1)} async-done(((bf16[512,128]{1,0:T(8,128)(2,1)}), bf16[512,128]{1,0:T(8,128)(2,1)}) %all-reduce.9.cloned.1.call-update) | async-done | bytes 131088 | tf_op jit(solution)/shard_map/psum | solution.py:14
  422.9 10.9 %all-to-all-start.3 = ((bf16[64,128,128]{2,1,0:T(8,128)(2,1)}), bf16[64,128,128]{2,1,0:T(8,128)(2,1)S(1)}, u32[]{:S(2)}, u32[]{:S(2)}) async-start(bf16[64,128,128]{2,1,0:T(8,128)(2,1)} %broadcast_select_fusion.1), calls=%async_computation.3 | async-start | bytes 4194304 | tf_op jit(solution)/shard_map/all_to_all | solution.py:33
  435.4 49.7 %all-to-all-done.3 = bf16[64,128,128]{2,1,0:T(8,128)(2,1)S(1)} async-done(((bf16[64,128,128]{2,1,0:T(8,128)(2,1)}), bf16[64,128,128]{2,1,0:T(8,128)(2,1)S(1)}, u32[]{:S(2)}, u32[]{:S(2)}) %all-to-all-start.3) | async-done | bytes 2097184 | tf_op jit(solution)/shard_map/all_to_all | solution.py:33
  485.0 2.1 gather_fusion.6
  487.1 8.1 %fusion.14 = f32[56,128,128]{1,2,0:T(8,128)} fusion(bf16[56,128,128]{2,1,0:T(8,128)(2,1)} %gather_fusion.6, f32[1,1,56,128,128]{4,3,2,1,0:T(8,128)} %param.10), kind=kOutput, calls=%fused_computation.23 | convolution fusion | flops 1409286144 | bytes 9175040 | tf_op jit(solution)/shard_map/jab,jbe->jae/dot_general | solution.py:35
  495.3 4.6 copy.43
  499.9 3.3 fusion.29
  505.3 71.2 %all-reduce.11.cloned.1.call-done = bf16[512,128]{1,0:T(8,128)(2,1)} async-done(((bf16[512,128]{1,0:T(8,128)(2,1)}), bf16[512,128]{1,0:T(8,128)(2,1)}) %all-reduce.11.cloned.1.call-update) | async-done | bytes 131088 | tf_op jit(solution)/shard_map/psum | solution.py:14
  579.8 11.0 %all-to-all-start.4 = ((bf16[64,128,128]{2,1,0:T(8,128)(2,1)}), bf16[64,128,128]{2,1,0:T(8,128)(2,1)S(1)}, u32[]{:S(2)}, u32[]{:S(2)}) async-start(bf16[64,128,128]{2,1,0:T(8,128)(2,1)} %broadcast_select_fusion), calls=%async_computation.4 | async-start | bytes 4194304 | tf_op jit(solution)/shard_map/all_to_all | solution.py:33
  593.4 48.8 %all-to-all-done.4 = bf16[64,128,128]{2,1,0:T(8,128)(2,1)S(1)} async-done(((bf16[64,128,128]{2,1,0:T(8,128)(2,1)}), bf16[64,128,128]{2,1,0:T(8,128)(2,1)S(1)}, u32[]{:S(2)}, u32[]{:S(2)}) %all-to-all-start.4) | async-done | bytes 2097184 | tf_op jit(solution)/shard_map/all_to_all | solution.py:33
  642.1 2.1 gather_fusion.8
  644.2 8.1 %fusion.17 = f32[56,128,128]{1,2,0:T(8,128)} fusion(bf16[56,128,128]{2,1,0:T(8,128)(2,1)} %gather_fusion.8, f32[1,1,56,128,128]{4,3,2,1,0:T(8,128)} %param.10), kind=kOutput, calls=%fused_computation.24 | convolution fusion | flops 1409286144 | bytes 9175040 | tf_op jit(solution)/shard_map/jab,jbe->jae/dot_general | solution.py:35
  652.4 4.6 copy.46
  657.0 3.3 fusion.27
  (64 shorter events, 30.0 us)
Async XLA Ops:
  7.2 18.6 %copy-start = (f32[4,128,128]{2,1,0:T(8,128)S(1)}, f32[4,128,128]{2,1,0:T(8,128)}, u32[]{:S(2)}) copy-start(f32[4,128,128]{2,1,0:T(8,128)} %param.9) | copy-start | bytes 786436
  10.9 22.4 %all-to-all-start = ((s32[64,1,1]{2,1,0:T(1,128)}), s32[64,1,1]{2,1,0:T(1,128)S(1)}, u32[]{:S(2)}, u32[]{:S(2)}) async-start(s32[64,1,1]{2,1,0:T(1,128)} %copy.35), calls=%async_computation | async-start | bytes 65536 | tf_op jit(solution)/shard_map/all_to_all | solution.py:51
  24.7 82.5 %all-reduce.5.cloned.1.call-start = ((), (), s32[]{:S(2)}) async-start(), calls=%async_computation.5 | async-start | bytes 262144 | tf_op jit(solution)/shard_map/psum | solution.py:14
  110.7 11.1 %copy-start.6 = (f32[1,512,128]{2,1,0:T(8,128)S(1)}, f32[1,512,128]{2,1,0:T(8,128)}, u32[]{:S(2)}) copy-start(f32[1,512,128]{2,1,0:T(8,128)} %param.8) | copy-start | bytes 786436
  110.7 62.3 %all-to-all-start.1 = ((bf16[64,128,128]{2,1,0:T(8,128)(2,1)}), bf16[64,128,128]{2,1,0:T(8,128)(2,1)S(1)}, u32[]{:S(2)}, u32[]{:S(2)}) async-start(bf16[64,128,128]{2,1,0:T(8,128)(2,1)} %broadcast_select_fusion.3), calls=%async_computation.1 | async-start | bytes 4194304 | tf_op jit(solution)/shard_map/all_to_all | solution.py:33
  121.7 141.8 %all-reduce.7.cloned.1.call-start = ((), (), s32[]{:S(2)}) async-start(), calls=%async_computation.6 | async-start | bytes 262144 | tf_op jit(solution)/shard_map/psum | solution.py:14
  121.8 69.4 %collective-permute-start = (f32[512,128]{1,0:T(8,128)S(1)}, f32[512,128]{1,0:T(8,128)S(1)}, u32[]{:S(2)}, u32[]{:S(2)}) collective-permute-start(f32[512,128]{1,0:T(8,128)S(1)} %bitcast.128), channel_id=1, source_target_pairs={{64,0},{128,64},{192,128},{256,192},{320,256},{384,320},{448,384},... | collective-permute-start | bytes 786440 | tf_op jit(solution)/shard_map/ppermute | solution.py:20
  183.1 4.6 copy-start.7
  187.8 3.4 copy-start.5
  266.9 62.1 %all-to-all-start.2 = ((bf16[64,128,128]{2,1,0:T(8,128)(2,1)}), bf16[64,128,128]{2,1,0:T(8,128)(2,1)S(1)}, u32[]{:S(2)}, u32[]{:S(2)}) async-start(bf16[64,128,128]{2,1,0:T(8,128)(2,1)} %broadcast_select_fusion.2), calls=%async_computation.2 | async-start | bytes 4194304 | tf_op jit(solution)/shard_map/all_to_all | solution.py:33
  277.8 141.7 %all-reduce.9.cloned.1.call-start = ((), (), s32[]{:S(2)}) async-start(), calls=%async_computation.7 | async-start | bytes 262144 | tf_op jit(solution)/shard_map/psum | solution.py:14
  277.8 69.3 %collective-permute-start.1 = (f32[512,128]{1,0:T(8,128)S(1)}, f32[512,128]{1,0:T(8,128)S(1)}, u32[]{:S(2)}, u32[]{:S(2)}) collective-permute-start(f32[512,128]{1,0:T(8,128)S(1)} %get-tuple-element.7), channel_id=1, source_target_pairs={{64,0},{128,64},{192,128},{256,192},{320,256},{384,320},{448,384},... | collective-permute-start | bytes 786440 | tf_op jit(solution)/shard_map/ppermute | solution.py:20
  422.9 62.2 %all-to-all-start.3 = ((bf16[64,128,128]{2,1,0:T(8,128)(2,1)}), bf16[64,128,128]{2,1,0:T(8,128)(2,1)S(1)}, u32[]{:S(2)}, u32[]{:S(2)}) async-start(bf16[64,128,128]{2,1,0:T(8,128)(2,1)} %broadcast_select_fusion.1), calls=%async_computation.3 | async-start | bytes 4194304 | tf_op jit(solution)/shard_map/all_to_all | solution.py:33
  433.8 142.6 %all-reduce.11.cloned.1.call-start = ((), (), s32[]{:S(2)}) async-start(), calls=%async_computation.8 | async-start | bytes 262144 | tf_op jit(solution)/shard_map/psum | solution.py:14
  433.9 69.3 %collective-permute-start.2 = (f32[512,128]{1,0:T(8,128)S(1)}, f32[512,128]{1,0:T(8,128)}, u32[]{:S(2)}, u32[]{:S(2)}) collective-permute-start(f32[512,128]{1,0:T(8,128)S(1)} %get-tuple-element.5), channel_id=1, source_target_pairs={{64,0},{128,64},{192,128},{256,192},{320,256},{384,320},{448,384},... | collective-permute-start | bytes 786440 | tf_op jit(solution)/shard_map/ppermute | solution.py:20
  579.8 12.6 %copy-start.1 = (bf16[512,128]{1,0:T(8,128)(2,1)S(1)}, bf16[512,128]{1,0:T(8,128)(2,1)}, u32[]{:S(2)}) copy-start(bf16[512,128]{1,0:T(8,128)(2,1)} %all-reduce.5.cloned.1.call-done) | copy-start | bytes 393220
  579.8 12.6 %copy-start.2 = (bf16[512,128]{1,0:T(8,128)(2,1)S(1)}, bf16[512,128]{1,0:T(8,128)(2,1)}, u32[]{:S(2)}) copy-start(bf16[512,128]{1,0:T(8,128)(2,1)} %all-reduce.7.cloned.1.call-done) | copy-start | bytes 393220
  579.8 12.6 %copy-start.3 = (bf16[512,128]{1,0:T(8,128)(2,1)S(1)}, bf16[512,128]{1,0:T(8,128)(2,1)}, u32[]{:S(2)}) copy-start(bf16[512,128]{1,0:T(8,128)(2,1)} %all-reduce.9.cloned.1.call-done) | copy-start | bytes 393220
  579.8 12.7 %copy-start.4 = (bf16[512,128]{1,0:T(8,128)(2,1)S(1)}, bf16[512,128]{1,0:T(8,128)(2,1)}, u32[]{:S(2)}) copy-start(bf16[512,128]{1,0:T(8,128)(2,1)} %all-reduce.11.cloned.1.call-done) | copy-start | bytes 393220
  579.8 62.3 %all-to-all-start.4 = ((bf16[64,128,128]{2,1,0:T(8,128)(2,1)}), bf16[64,128,128]{2,1,0:T(8,128)(2,1)S(1)}, u32[]{:S(2)}, u32[]{:S(2)}) async-start(bf16[64,128,128]{2,1,0:T(8,128)(2,1)} %broadcast_select_fusion), calls=%async_computation.4 | async-start | bytes 4194304 | tf_op jit(solution)/shard_map/all_to_all | solution.py:33
  590.9 69.4 %collective-permute-start.3 = (f32[512,128]{1,0:T(8,128)S(1)}, f32[512,128]{1,0:T(8,128)S(1)}, u32[]{:S(2)}, u32[]{:S(2)}) collective-permute-start(f32[512,128]{1,0:T(8,128)S(1)} %get-tuple-element.3), channel_id=1, source_target_pairs={{64,0},{128,64},{192,128},{256,192},{320,256},{384,320},{448,384},... | collective-permute-start | bytes 786440 | tf_op jit(solution)/shard_map/ppermute | solution.py:20
Sparse Core Ops, SparseCore 0:
  28.4 78.7 all-reduce.4
  192.4 70.9 all-reduce.6
  348.4 70.9 all-reduce.8
  505.4 70.9 all-reduce.10
where the time goes:
time: 669 us; the launch traced here: 668 us
  waiting for transfers between devices  490 us (73%)
  starting transfers between devices  63.6 us (10%)
  matrix products  50.1 us (7%)
  local copies, waits for them, and re-layouts  36.4 us (5%)
  between operations  14 us (2%)
  other arithmetic  13.9 us (2%)
    psum x4, waiting for transfers between devices, broadcast(): return lax.psum(jnp.where(mine, x, jnp.zeros_like(x)), axis)  285 us
    all_to_all x4, waiting for transfers between devices, lag_part(): lax.all_to_all(outgoing, 'patch', split_axis=0, concat_axis=0, tiled=True)  198 us
    all_to_all x4, starting transfers between devices, lag_part(): lax.all_to_all(outgoing, 'patch', split_axis=0, concat_axis=0, tiled=True)  43.9 us
    dot_general x4, matrix products, lag_part(): jnp.einsum('jab,jbe->jae', weights, picked, precision=lax.Precision.HIGHEST)  32.6 us
    dot_general x4, local copies, waits for them, and re-layouts, lag_part(): jnp.einsum('jab,jbe->jae', weights, picked, precision=lax.Precision.HIGHEST)  18.4 us
    all_to_all x1, starting transfers between devices, body(): lax.all_to_all(wanted.reshape(patches, 1), 'patch', split_axis=0, concat_...  13.9 us
  transfers between devices with their start and end apart: 13, of which 9 were waited for; matrix products, arithmetic and copies ran while one was open for 12% of the time, Pallas kernels for 0%

commit v1 on v0

v1 whole, which is shorter than its diff:
```python
import jax
import jax.numpy as jnp
from jax import lax
from jax.experimental import pallas as pl
from jax.experimental.pallas import tpu as pltpu
from jax.sharding import PartitionSpec as P

EXC = 128
B = 128
NB = 4
OWN = NB * B
STEPS = 4
LIST = 56
NX, NZ, NY = 4, 8, 8
MESH = pl.DeviceIdType.MESH

ORDER = (0, 1, 7, 2, 6, 3, 5, 4)
GROUPS = ((0, 1), (1, 3), (3, 5), (5, 7), (7, 8))
HALF = OWN // 2


def kernel(enc, inc, pend, sinv, want, zmat, cur_out, ahead_out,
           zf, w, items, pick, sbuf, rbuf, part, shift, acc, wanted, onehot,
           load_sem, bc_r, z_r, x_r, r_r, sh_r, q_r, bc_s, z_s, x_s, r_s, sh_s, q_s):
    y = lax.axis_index("lag")
    p = lax.axis_index("patch")
    c = lax.rem(p, 2)
    x = lax.rem(lax.div(p, 2), NX)
    z = lax.div(p, 2 * NX)

    def at(dx=0, dz=0, core=None):
        core = c if core is None else core
        return lax.rem(z + dz + NZ, NZ) * (2 * NX) + lax.rem(x + dx, NX) * 2 + core

    def dev(patch, lag=None):
        return {"lag": y if lag is None else lag, "patch": patch}

    up, down = lax.rem(y + 1, NY), lax.rem(y + NY - 1, NY)
    partner = 1 - c
    peers = [dev(at(dz=1)), dev(at(dz=-1)), dev(at(core=partner)), dev(p, up), dev(p, down)]
    peers += [dev(at(dx=dx, core=k)) for dx in (1, 2, 3) for k in (0, 1)]

    load = pltpu.make_async_copy(zmat.at[0, 0], zf, load_sem)
    load.start()

    barrier = pltpu.get_barrier_semaphore()
    for peer in peers:
        pl.semaphore_signal(barrier, inc=1, device_id=peer, device_id_type=MESH)
    pl.semaphore_wait(barrier, len(peers))

    def remote(src, dst, ssem, rsem, where):
        return pltpu.make_async_remote_copy(
            src_ref=src, dst_ref=dst, send_sem=ssem, recv_sem=rsem,
            device_id=where, device_id_type=MESH)

    def asks():
        out = [remote(want.at[1 - c], wanted.at[c], q_s.at[0], q_r.at[c], dev(at(core=partner)))]
        for dx in (1, 2, 3):
            for k in (0, 1):
                t, back = dx * 2 + k, (NX - dx) * 2
                out.append(remote(want.at[t], wanted.at[back + c], q_s.at[t - 1], q_r.at[back + c],
                                  dev(at(dx=dx, core=k))))
        return out

    for copy in asks():
        copy.start()

    part[0] = pend[0]

    def step(n, carry):
        def bcast(k, lag, sem):
            rows = pl.ds(k * HALF, HALF)
            return remote(items.at[n, 0, rows], items.at[n, 0, rows], bc_s.at[sem, k], bc_r.at[n, k],
                          dev(p, lag))

        def ring(d_from, d_to, k, dz):
            rows = pl.ds(k * HALF, HALF)
            return remote(items.at[n, d_from, rows], items.at[n, d_to, rows], z_s.at[d_to, k],
                          z_r.at[n, d_to, k], dev(at(dz=dz)))

        def sends(g):
            p0, p1 = GROUPS[g]
            span = pl.ds(p0, p1 - p0)
            out = [remote(sbuf.at[0, span], pick.at[n, span, pl.ds(pl.multiple_of(c * B, B), B)],
                          x_s.at[g, 0], x_r.at[n, g, c], dev(at(core=partner)))]
            for dx in (1, 3):
                for k in (0, 1):
                    t, back = dx * 2 + k, (NX - dx) * 2 + c
                    out.append(remote(
                        sbuf.at[t, span], pick.at[n, span, pl.ds(pl.multiple_of(back * B, B), B)],
                        x_s.at[g, t - 1], x_r.at[n, g, back], dev(at(dx=dx, core=k))))
            for k, dx in ((0, 1), (1, 3)):
                out.append(remote(sbuf.at[4 + k, span], rbuf.at[n, k, span], x_s.at[g, 3 + k],
                                  r_r.at[n, g, k], dev(at(dx=dx))))
            return out

        def relays(g):
            p0, p1 = GROUPS[g]
            span = pl.ds(p0, p1 - p0)
            rows = pl.ds(pl.multiple_of((4 + c) * B, B), B)
            return [remote(rbuf.at[n, k, span], pick.at[n, span, rows], r_s.at[g, k],
                           x_r.at[n, g, 4 + c], dev(at(dx=dx, core=k))) for k, dx in ((0, 1), (1, 3))]

        def select(pos):
            whole = items[n, ORDER[pos]].reshape(NB, B // 16, 16, EXC)

            def choose(t):
                total = whole[0] * onehot[t, pos * NB][None]
                for k in range(1, NB):
                    total = total + whole[k] * onehot[t, pos * NB + k][None]
                return total.reshape(B, EXC)

            pick[n, pos, pl.ds(pl.multiple_of(c * B, B), B), :] = choose(c)
            sbuf[0, pos] = choose(partner)
            for t in range(2, 8):
                sbuf[t, pos] = choose(t)

        def pass_on(g):
            for pos in range(*GROUPS[g]):
                select(pos)
            for copy in sends(g):
                copy.start()

        def relay(g):
            p0, p1 = GROUPS[g]
            span = pl.ds(p0, p1 - p0)
            for k, copy in enumerate(relays(g)):
                remote(rbuf.at[n, k, span], rbuf.at[n, k, span], r_s.at[g, k], r_r.at[n, g, k],
                       dev(p, up)).wait_recv()
                copy.start()

        def apply(g):
            p0, p1 = GROUPS[g]
            span = pl.ds(p0, p1 - p0)
            for s in range(8):
                block = pick.at[n, span, pl.ds(s * B, B)]
                wait = remote(block, block, x_s.at[g, 0], x_r.at[n, g, s], dev(p, up)).wait_recv
                if s < 2:
                    pl.when(c != s)(wait)
                else:
                    wait()
            for pos in range(p0, p1):
                term = jnp.dot(w[pos], pick[n, pos], preferred_element_type=jnp.float32)
                if pos == 0:
                    acc[...] = term
                else:
                    acc[...] += term

        first = n == 0

        @pl.when(y == 0)
        def _():
            for k in range(NB):
                rows = slice(k * B, (k + 1) * B)
                excess = inc[n, rows].astype(jnp.float32) - part[n, rows]
                solved = jnp.dot(sinv[k], excess, precision=lax.Precision.HIGHEST,
                                 preferred_element_type=jnp.float32)
                items[n, 0, rows] = solved.astype(jnp.bfloat16)

        goes_up = [y <= 3, y <= 2]
        goes_down = [(y == 0) | (y >= 6), (y == 0) | (y >= 5)]
        for k in range(2):
            pl.when(y != 0)(bcast(k, up, 0).wait_recv)
            pl.when(goes_up[k])(bcast(k, up, 0).start)
            pl.when(goes_down[k])(bcast(k, down, 1).start)
            ring(0, 1, k, 1).start()
            ring(0, 7, k, -1).start()

        @pl.when(first)
        def _():
            for t in range(8):
                if t < 2:
                    pl.when(c != t)(remote(wanted.at[t], wanted.at[t], q_s.at[0], q_r.at[t], dev(p, up)).wait_recv)
                else:
                    remote(wanted.at[t], wanted.at[t], q_s.at[0], q_r.at[t], dev(p, up)).wait_recv()
            wanted[c] = want[c]

            def spread(t, carry):
                for r in range(NB * NZ):
                    onehot[t, r] = jnp.broadcast_to(wanted[t, pl.ds(r, 1), :], (16, EXC)).astype(jnp.bfloat16)
                return carry

            lax.fori_loop(0, 8, spread, 0)

        pass_on(0)
        cur_out[n] = items[n, 0]
        move = remote(part.at[n], shift.at[n], sh_s, sh_r.at[n], dev(p, down))
        pl.when(y != 0)(move.start)

        for k in range(2):
            ring(0, 1, k, 1).wait_recv()
            ring(1, 2, k, 1).start()
            ring(0, 7, k, -1).wait_recv()
            ring(7, 6, k, -1).start()
        pass_on(1)
        relay(0)
        for k in range(2):
            ring(1, 2, k, 1).wait_recv()
            ring(2, 3, k, 1).start()
            ring(7, 6, k, -1).wait_recv()
            ring(6, 5, k, -1).start()
        pass_on(2)
        relay(1)
        for k in range(2):
            ring(2, 3, k, 1).wait_recv()
            ring(6, 5, k, -1).wait_recv()
            if k == 0:
                ring(3, 4, 0, 1).start()
            else:
                ring(5, 4, 1, -1).start()
        pass_on(3)
        relay(2)
        ring(3, 4, 0, 1).wait_recv()
        ring(5, 4, 1, -1).wait_recv()
        pass_on(4)

        @pl.when(first)
        def _():
            pltpu.make_async_copy(zmat.at[0, 0], zf, load_sem).wait()

            def place(s, carry):
                code = enc[s]
                row = jnp.where(code < 0, -1, (code >> 2) & 3)
                block = zf[jnp.maximum(code, 0) >> 4].astype(jnp.bfloat16)
                pos, col = lax.div(s, 8), lax.rem(s, 8)
                for r in range(NB):
                    keep = jnp.where(row == r, 1.0, 0.0).astype(jnp.bfloat16)
                    w[pos, pl.ds(r * B, B), pl.ds(pl.multiple_of(col * B, B), B)] = block * keep
                return carry

            lax.fori_loop(0, 64, place, 0)

        relay(3)
        apply(0)
        relay(4)
        for g in range(1, 5):
            apply(g)

        pl.when(y != NY - 1)(move.wait_recv)

        @pl.when(y != NY - 1)
        def _():
            part[n + 1] = acc[...] + shift[n]

        @pl.when(y == NY - 1)
        def _():
            part[n + 1] = acc[...]

        for k in range(2):
            pl.when(goes_up[k])(bcast(k, up, 0).wait_send)
            pl.when(goes_down[k])(bcast(k, down, 1).wait_send)
            for d_from, d_to, dz in ((0, 1, 1), (1, 2, 1), (2, 3, 1), (0, 7, -1), (7, 6, -1), (6, 5, -1)):
                ring(d_from, d_to, k, dz).wait_send()
        ring(3, 4, 0, 1).wait_send()
        ring(5, 4, 1, -1).wait_send()
        for g in range(5):
            for copy in sends(g) + relays(g):
                copy.wait_send()
        pl.when(y != 0)(move.wait_send)
        return carry

    lax.fori_loop(0, STEPS, step, 0)
    for copy in asks():
        copy.wait_send()
    ahead_out[0] = part[STEPS]


def body(incident, pending, self_inverse, retarded, block_rows, block_sources, owner_map):
    p = lax.axis_index("patch")
    x, z = (p // 2) % NX, p // (2 * NX)
    row = block_rows[0, 0]
    source = block_sources[0, 0]
    live = source >= 0
    storage = owner_map[jnp.maximum(source, 0)]
    owner, local = storage // NB, storage % NB
    d = (z - owner // (2 * NX)) % NZ
    pos = jnp.where(d == 0, 0, jnp.where(d <= 3, 2 * d - 1, jnp.where(d == 4, 7, 2 * (NZ - d))))
    column = ((owner // 2) % NX - x) % NX * 2 + owner % 2
    slot = pos * 8 + column
    code = jnp.arange(LIST, dtype=jnp.int32) * 16 + row * 4 + local
    hit = (slot[None, :] == jnp.arange(64)[:, None]) & live[None, :]
    enc = jnp.max(jnp.where(hit, code[None, :], -1), axis=1).astype(jnp.int32)
    picked = jnp.maximum(enc, 0) % NB
    wants = (picked.reshape(NZ, 8).T[:, :, None] == jnp.arange(NB)).astype(jnp.float32)
    want = jnp.broadcast_to(wants.reshape(8, NZ * NB)[:, :, None], (8, NZ * NB, EXC))

    vmem = pl.BlockSpec(memory_space=pltpu.VMEM)
    dma = pltpu.SemaphoreType.DMA
    return pl.pallas_call(
        kernel,
        out_shape=(jax.ShapeDtypeStruct((STEPS, OWN, EXC), jnp.bfloat16),
                   jax.ShapeDtypeStruct((1, OWN, EXC), jnp.float32)),
        in_specs=[pl.BlockSpec(memory_space=pltpu.SMEM), vmem, vmem, vmem, vmem,
                  pl.BlockSpec(memory_space=pl.ANY)],
        out_specs=(vmem, vmem),
        scratch_shapes=[
            pltpu.VMEM((LIST, B, B), jnp.float32),
            pltpu.VMEM((NZ, OWN, 8 * B), jnp.bfloat16),
            pltpu.VMEM((STEPS, NZ, OWN, EXC), jnp.bfloat16),
            pltpu.VMEM((STEPS, NZ, 8 * B, EXC), jnp.bfloat16),
            pltpu.VMEM((8, NZ, B, EXC), jnp.bfloat16),
            pltpu.VMEM((STEPS, 2, NZ, B, EXC), jnp.bfloat16),
            pltpu.VMEM((STEPS + 1, OWN, EXC), jnp.float32),
            pltpu.VMEM((STEPS, OWN, EXC), jnp.float32),
            pltpu.VMEM((OWN, EXC), jnp.float32),
            pltpu.VMEM((8, NZ * NB, EXC), jnp.float32),
            pltpu.VMEM((8, NZ * NB, 16, EXC), jnp.bfloat16),
            dma, dma((STEPS, 2)), dma((STEPS, NZ, 2)), dma((STEPS, 5, 8)), dma((STEPS, 5, 2)),
            dma((STEPS,)), dma((8,)),
            dma((2, 2)), dma((NZ, 2)), dma((5, 7)), dma((5, 2)), dma, dma((8,)),
        ],
        compiler_params=pltpu.CompilerParams(collective_id=0, has_side_effects=True,
                                             vmem_limit_bytes=60 * 1024 * 1024),
    )(enc, incident, pending, self_inverse, want, retarded)


def solution(mesh):
    in_specs = (
        P(None, "patch", None),
        P("lag", "patch", None),
        P("patch", None, None),
        P("lag", "patch", None, None, None),
        P("lag", "patch", None),
        P("lag", "patch", None),
        P(),
    )
    out_specs = (P(None, "patch", None), P("lag", "patch", None))
    return jax.shard_map(body, mesh=mesh, in_specs=in_specs, out_specs=out_specs, check_vma=False)
```

time: 669 us -> 162 us (0.24)
  the two profiles are of different devices: /device:TPU:2 before, /device:TPU:32 now
where the time goes in v1:
time: 162 us
  Pallas kernels  154 us (95%)
  local copies, waits for them, and re-layouts  5.34 us (3%)
  other arithmetic  2.14 us (1%)
    pallas_call x1, Pallas kernels, body(): pl.pallas_call(kernel, out_shape=(jax.ShapeDtypeStruct((STEPS, OWN, EXC),...  154 us
    unnamed x6, local copies, waits for them, and re-layouts  3.55 us

profile of v1, /device:TPU:32, one launch (start us, length us, event | category | flops | bytes accessed | tf_op | source)
XLA Modules:
  0.0 162.0 jit_solution(3838398819951358186)
XLA Ops:
  0.6 0.0 copy-start
  0.7 0.7 compare_bitcast_fusion
  1.3 0.7 maximum_bitcast_fusion
  2.0 0.0 copy-done
  2.0 0.8 gather_fusion
  2.8 0.7 fusion.4
  3.5 0.1 select_reduce_fusion.enc
  3.6 0.0 copy-start.1
  3.6 0.1 rem.204
  3.7 0.1 eq.68
  3.8 0.1 copy.12
  3.9 0.8 broadcast_in_dim.19.want
  4.7 0.0 copy-done.1
  4.7 153.8 %shard_map.86 = (bf16[4,512,128]{2,1,0:T(8,128)(2,1)}, f32[1,512,128]{2,1,0:T(8,128)}) custom-call(s32[64]{0:T(128)} %copy-done.1, bf16[4,512,128]{2,1,0:T(8,128)(2,1)} %inc.1, f32[1,512,128]{2,1,0:T(8,128)} %pend.1, f32[4,128,128]{2,1,0:T(8,128)} %sinv.1, f32[8,32,128]{2,1,0:T(8,128)} %broadcast_in_dim.19.want, f32[1,1,56,128,128]{4,3,2,1,0:T(8,128)} %zmat.1), custom_call_target="tpu_custom_call" | custom-call | tf_op jit(solution)/shard_map/pallas_call | solution.py:289
  158.5 1.9 %copy.15 = bf16[4,512,128]{2,1,0:T(8,128)(2,1)} copy(bf16[4,512,128]{2,1,0:T(8,128)(2,1)} %get-tuple-element.6) | data formatting | bytes 1048576
  160.3 1.7 %copy.16 = f32[1,512,128]{2,1,0:T(8,128)} copy(f32[1,512,128]{2,1,0:T(8,128)} %get-tuple-element.7) | data formatting | bytes 524288
  (6 shorter events, 0.0 us)
Async XLA Ops:
  0.6 1.4 copy-start
  3.6 1.0 copy-start.1

commit v2 on v1

v2 whole, which is shorter than its diff:
```python
import jax
import jax.numpy as jnp
from jax import lax
from jax.experimental import pallas as pl
from jax.experimental.pallas import tpu as pltpu
from jax.sharding import PartitionSpec as P

EXC = 128
B = 128
NB = 4
OWN = NB * B
STEPS = 4
LIST = 56
SRC = 256
NX, NZ, NY = 4, 8, 8
MESH = pl.DeviceIdType.MESH

ORDER = (0, 1, 7, 2, 6, 3, 5, 4)
GROUPS = ((0, 1), (1, 3), (3, 5), (5, 7), (7, 8))
MAIN, SLAB = 96, 32


def kernel(enc, inc, pend, sinv, zmat, cur_out, ahead_out,
           zf, w, items, slabs, pick, sbuf, pbuf, qbuf, rbuf, part, shift, acc, want, wanted, wanted2, onehot,
           load_sem, bc_r, z_r, s_r, x_r, r_r, p_r, sh_r, q_r,
           bc_s, z_s, s_s, x_s, r_s, p_s, sh_s, q_s):
    y = lax.axis_index("lag")
    p = lax.axis_index("patch")
    c = lax.rem(p, 2)
    x = lax.rem(lax.div(p, 2), NX)
    z = lax.div(p, 2 * NX)

    def at(dx=0, dz=0, core=None):
        core = c if core is None else core
        return lax.rem(z + dz + NZ, NZ) * (2 * NX) + lax.rem(x + dx, NX) * 2 + core

    def dev(patch, lag=None):
        return {"lag": y if lag is None else lag, "patch": patch}

    up, down = lax.rem(y + 1, NY), lax.rem(y + NY - 1, NY)
    partner = 1 - c
    mate = dev(at(core=partner))
    peers = [dev(at(dz=1)), dev(at(dz=-1)), mate, dev(p, up), dev(p, down)]
    peers += [dev(at(dx=dx, core=k)) for dx in (1, 2, 3) for k in (0, 1)]

    load = pltpu.make_async_copy(zmat.at[0, 0], zf, load_sem)
    load.start()

    barrier = pltpu.get_barrier_semaphore()
    for peer in peers:
        pl.semaphore_signal(barrier, inc=1, device_id=peer, device_id_type=MESH)

    def ask(s, carry):
        pos, t = lax.div(s, 8), lax.rem(s, 8)
        local = jnp.maximum(enc[s], 0) & 3
        for k in range(NB):
            want[t, pl.ds(pos * NB + k, 1), :] = jnp.full((1, EXC), jnp.where(local == k, 1.0, 0.0), jnp.float32)
        return carry

    lax.fori_loop(0, 64, ask, 0)
    part[0] = pend[0]
    pl.semaphore_wait(barrier, len(peers))

    def remote(src, dst, ssem, rsem, where):
        return pltpu.make_async_remote_copy(
            src_ref=src, dst_ref=dst, send_sem=ssem, recv_sem=rsem,
            device_id=where, device_id_type=MESH)

    def arrives(ref, rsem):
        return remote(ref, ref, sh_s, rsem, mate).wait_recv

    def asks():
        out = [remote(want.at[partner], wanted.at[c], q_s.at[0], q_r.at[c], mate)]
        for dx in (1, 2, 3):
            out.append(remote(want.at[dx * 2 + partner], wanted2.at[dx - 1], q_s.at[6 + dx], q_r.at[7 + dx], mate))
            for k in (0, 1):
                t, back = dx * 2 + k, (NX - dx) * 2
                out.append(remote(want.at[t], wanted.at[back + c], q_s.at[t - 1], q_r.at[back + c],
                                  dev(at(dx=dx, core=k))))
        return out

    for copy in asks():
        copy.start()

    def step(n, carry):
        def mine(row):
            return pl.ds(pl.multiple_of(row * B, B), B)

        def bcast(i, lag, sem):
            piece = items.at[n, 0, i // 2, pl.ds((i % 2) * (B // 2), B // 2)]
            return remote(piece, piece, bc_s.at[sem, i], bc_r.at[n, i], dev(p, lag))

        def ring(d_from, d_to, k, dz):
            half = pl.ds(2 * k, 2)
            return remote(items.at[n, d_from, half], items.at[n, d_to, half], z_s.at[d_to, k],
                          z_r.at[n, d_to, k], dev(at(dz=dz)))

        def slab_start():
            return [remote(items.at[n, 0, :, pl.ds(MAIN, SLAB)], slabs.at[n, 0, NX - dx - 1], s_s.at[0, dx - 1],
                           s_r.at[n, 0, NX - dx - 1], dev(at(dx=dx))) for dx in (2, 1, 3)]

        def slab_ring(d_from, d_to, k, dz):
            half = pl.ds(2 * k, 2)
            return remote(slabs.at[n, d_from, :, half], slabs.at[n, d_to, :, half], s_s.at[d_to, k],
                          s_r.at[n, d_to, k], dev(at(dz=dz)))

        def span_of(g):
            p0, p1 = GROUPS[g]
            return pl.ds(p0, p1 - p0)

        def sends(g):
            span = span_of(g)
            out = []
            for k, dx in ((0, 1), (1, 3)):
                out.append(remote(sbuf.at[2 + k, span], rbuf.at[n, k, span], x_s.at[g, 3 + k],
                                  r_r.at[n, g, k], dev(at(dx=dx))))
            for dx in (1, 3):
                for k in (0, 1):
                    t, back = dx * 2 + k, (NX - dx) * 2 + c
                    out.append(remote(
                        sbuf.at[t - 2, span], pick.at[n, span, pl.ds(pl.multiple_of(back * B, B), MAIN)],
                        x_s.at[g, t - 1], x_r.at[n, g, back], dev(at(dx=dx, core=k))))
            out.append(remote(pbuf.at[span], pick.at[n, span, mine(c)], x_s.at[g, 0], x_r.at[n, g, c], mate))
            return out

        def slab_sends(g):
            span = span_of(g)
            return [remote(qbuf.at[dx - 1, span],
                           pick.at[n, span, pl.ds(pl.multiple_of((dx * 2 + c) * B + MAIN, SLAB), SLAB)],
                           p_s.at[g, dx - 1], p_r.at[n, g, dx - 1], mate) for dx in (1, 2, 3)]

        def relays(g):
            span = span_of(g)
            rows = pl.ds(pl.multiple_of((4 + c) * B, B), MAIN)
            return [remote(rbuf.at[n, k, span], pick.at[n, span, rows], r_s.at[g, k],
                           x_r.at[n, g, 4 + c], dev(at(dx=dx, core=k))) for k, dx in ((0, 1), (1, 3))]

        def choose(blocks, table, pos, rows):
            total = None
            for k in range(NB):
                term = blocks[k].reshape(rows // 16, 16, EXC) * onehot[table, pos * NB + k][None]
                total = term if total is None else total + term
            return total.reshape(rows, EXC)

        def pass_on(g):
            for pos in range(*GROUPS[g]):
                whole = [items[n, ORDER[pos], k] for k in range(NB)]
                head = [block[:MAIN] for block in whole]
                for t in (4, 5, 2, 3, 6, 7):
                    sbuf[t - 2, pos] = choose(head, t, pos, MAIN)
                pbuf[pos] = choose(whole, partner, pos, B)
                pick[n, pos, mine(c), :] = choose(whole, c, pos, B)
            for copy in sends(g):
                copy.start()

        def slab_pass(g):
            for pos in range(*GROUPS[g]):
                for dx in (1, 2, 3):
                    blocks = [slabs[n, ORDER[pos], dx - 1, k] for k in range(NB)]
                    qbuf[dx - 1, pos] = choose(blocks, 11 + dx - 1, pos, SLAB)
                    rows = pl.ds(pl.multiple_of((dx * 2 + c) * B + MAIN, SLAB), SLAB)
                    pick[n, pos, rows, :] = choose(blocks, 8 + dx - 1, pos, SLAB)
            for copy in slab_sends(g):
                copy.start()

        def relay(g):
            for k, copy in enumerate(relays(g)):
                arrives(rbuf.at[n, k, span_of(g)], r_r.at[n, g, k])()
                copy.start()

        def apply(g):
            span = span_of(g)
            for s in range(8):
                if s < 2:
                    pl.when(c != s)(arrives(pick.at[n, span, pl.ds(s * B, B)], x_r.at[n, g, s]))
                else:
                    arrives(pick.at[n, span, pl.ds(s * B, MAIN)], x_r.at[n, g, s])()
            for dx in (1, 2, 3):
                rows = pl.ds(pl.multiple_of((dx * 2 + partner) * B + MAIN, SLAB), SLAB)
                arrives(pick.at[n, span, rows], p_r.at[n, g, dx - 1])()
            for pos in range(*GROUPS[g]):
                term = jnp.dot(w[pos], pick[n, pos], preferred_element_type=jnp.float32)
                if pos == 0:
                    acc[...] = term
                else:
                    acc[...] += term

        first = n == 0

        @pl.when(y == 0)
        def _():
            for k in range(NB):
                rows = slice(k * B, (k + 1) * B)
                excess = inc[n, rows].astype(jnp.float32) - part[n, rows]
                solved = jnp.dot(sinv[k], excess, precision=lax.Precision.HIGHEST,
                                 preferred_element_type=jnp.float32)
                items[n, 0, k] = solved.astype(jnp.bfloat16)

        goes_up = [y <= 3, y <= 2]
        goes_down = [(y == 0) | (y >= 6), (y == 0) | (y >= 5)]
        for i in range(8):
            piece = items.at[n, 0, i // 2, pl.ds((i % 2) * (B // 2), B // 2)]
            pl.when(y != 0)(arrives(piece, bc_r.at[n, i]))
            pl.when(goes_up[i // 4])(bcast(i, up, 0).start)
            pl.when(goes_down[i // 4])(bcast(i, down, 1).start)
            if i % 4 == 3:
                ring(0, 1, i // 4, 1).start()
                ring(0, 7, i // 4, -1).start()
        for copy in slab_start():
            copy.start()

        @pl.when(first)
        def _():
            for t in range(8):
                if t < 2:
                    pl.when(c != t)(arrives(wanted.at[t], q_r.at[t]))
                else:
                    arrives(wanted.at[t], q_r.at[t])()
            wanted[c] = want[c]
            for dx in (1, 2, 3):
                arrives(wanted2.at[dx - 1], q_r.at[7 + dx])()

            def line(rows):
                return jnp.broadcast_to(rows, (16, EXC)).astype(jnp.bfloat16)

            def spread(t, carry):
                for r in range(NB * NZ):
                    onehot[t, r] = line(wanted[t, pl.ds(r, 1), :])
                return carry

            def spread_slabs(i, carry):
                for r in range(NB * NZ):
                    onehot[8 + i, r] = line(want[i * 2 + 2 + c, pl.ds(r, 1), :])
                    onehot[11 + i, r] = line(wanted2[i, pl.ds(r, 1), :])
                return carry

            lax.fori_loop(0, 8, spread, 0)
            lax.fori_loop(0, 3, spread_slabs, 0)

        pass_on(0)
        cur_out[n] = items[n, 0].reshape(OWN, EXC)
        move = remote(part.at[n], shift.at[n], sh_s, sh_r.at[n], dev(p, down))
        pl.when(y != 0)(move.start)

        def hop(make, a, b, arrive):
            for k in range(2):
                make(a[0] - 1, a[0], k, 1).wait_recv()
                if arrive == 3:
                    if k == 0:
                        make(a[0], 4, 0, 1).start()
                else:
                    make(a[0], a[0] + 1, k, 1).start()
                make(b[0], b[0], k, -1).wait_recv()
                if arrive == 3:
                    if k == 1:
                        make(b[0], 4, 1, -1).start()
                else:
                    make(b[0], b[0] - 1, k, -1).start()

        hop(ring, (1,), (7,), 1)
        for i in range(3):
            arrives(slabs.at[n, 0, i], s_r.at[n, 0, i])()
        for k in range(2):
            slab_ring(0, 1, k, 1).start()
            slab_ring(0, 7, k, -1).start()
        pass_on(1)
        hop(ring, (2,), (6,), 2)
        relay(0)
        hop(slab_ring, (1,), (7,), 1)
        pass_on(2)
        slab_pass(0)
        hop(ring, (3,), (5,), 3)
        relay(1)
        pass_on(3)
        hop(slab_ring, (2,), (6,), 2)
        slab_pass(1)

        @pl.when(first)
        def _():
            pltpu.make_async_copy(zmat.at[0, 0], zf, load_sem).wait()

            def place(s, carry):
                code = enc[s]
                row = jnp.where(code < 0, -1, (code >> 2) & 3)
                block = zf[jnp.maximum(code, 0) >> 4].astype(jnp.bfloat16)
                pos, col = lax.div(s, 8), lax.rem(s, 8)
                for r in range(NB):
                    keep = jnp.where(row == r, 1.0, 0.0).astype(jnp.bfloat16)
                    w[pos, pl.ds(r * B, B), pl.ds(pl.multiple_of(col * B, B), B)] = block * keep
                return carry

            lax.fori_loop(0, 64, place, 0)

        relay(2)
        ring(3, 4, 0, 1).wait_recv()
        ring(5, 4, 1, -1).wait_recv()
        pass_on(4)
        apply(0)
        hop(slab_ring, (3,), (5,), 3)
        slab_pass(2)
        relay(3)
        apply(1)
        slab_pass(3)
        relay(4)
        apply(2)
        slab_ring(3, 4, 0, 1).wait_recv()
        slab_ring(5, 4, 1, -1).wait_recv()
        slab_pass(4)
        apply(3)
        apply(4)

        pl.when(y != NY - 1)(move.wait_recv)

        @pl.when(y != NY - 1)
        def _():
            part[n + 1] = acc[...] + shift[n]

        @pl.when(y == NY - 1)
        def _():
            part[n + 1] = acc[...]

        for i in range(8):
            pl.when(goes_up[i // 4])(bcast(i, up, 0).wait_send)
            pl.when(goes_down[i // 4])(bcast(i, down, 1).wait_send)
        for make in (ring, slab_ring):
            for k in range(2):
                for d_from, d_to, dz in ((0, 1, 1), (1, 2, 1), (2, 3, 1), (0, 7, -1), (7, 6, -1), (6, 5, -1)):
                    make(d_from, d_to, k, dz).wait_send()
            make(3, 4, 0, 1).wait_send()
            make(5, 4, 1, -1).wait_send()
        for copy in slab_start():
            copy.wait_send()
        for g in range(5):
            for copy in sends(g) + relays(g) + slab_sends(g):
                copy.wait_send()
        pl.when(y != 0)(move.wait_send)
        return carry

    lax.fori_loop(0, STEPS, step, 0)
    for copy in asks():
        copy.wait_send()
    ahead_out[0] = part[STEPS]


def body(incident, pending, self_inverse, retarded, block_rows, block_sources, owner_map):
    p = lax.axis_index("patch")
    x, z = (p // 2) % NX, p // (2 * NX)
    row = block_rows[0, 0]
    source = block_sources[0, 0]
    live = source >= 0
    storage = jnp.sum(jnp.where(source[:, None] == jnp.arange(SRC)[None, :], owner_map[None, :], 0), axis=1)
    owner, local = storage // NB, storage % NB
    d = (z - owner // (2 * NX)) % NZ
    pos = jnp.where(d == 0, 0, jnp.where(d <= 3, 2 * d - 1, jnp.where(d == 4, 7, 2 * (NZ - d))))
    column = ((owner // 2) % NX - x) % NX * 2 + owner % 2
    slot = pos * 8 + column
    code = jnp.arange(LIST, dtype=jnp.int32) * 16 + row * 4 + local
    hit = (slot[None, :] == jnp.arange(64)[:, None]) & live[None, :]
    enc = jnp.max(jnp.where(hit, code[None, :], -1), axis=1).astype(jnp.int32)
    vmem = pl.BlockSpec(memory_space=pltpu.VMEM)
    dma = pltpu.SemaphoreType.DMA
    return pl.pallas_call(
        kernel,
        out_shape=(jax.ShapeDtypeStruct((STEPS, OWN, EXC), jnp.bfloat16),
                   jax.ShapeDtypeStruct((1, OWN, EXC), jnp.float32)),
        in_specs=[pl.BlockSpec(memory_space=pltpu.SMEM), vmem, vmem, vmem,
                  pl.BlockSpec(memory_space=pl.ANY)],
        out_specs=(vmem, vmem),
        scratch_shapes=[
            pltpu.VMEM((LIST, B, B), jnp.float32),
            pltpu.VMEM((NZ, OWN, 8 * B), jnp.bfloat16),
            pltpu.VMEM((STEPS, NZ, NB, B, EXC), jnp.bfloat16),
            pltpu.VMEM((STEPS, NZ, NX - 1, NB, SLAB, EXC), jnp.bfloat16),
            pltpu.VMEM((STEPS, NZ, 8 * B, EXC), jnp.bfloat16),
            pltpu.VMEM((6, NZ, MAIN, EXC), jnp.bfloat16),
            pltpu.VMEM((NZ, B, EXC), jnp.bfloat16),
            pltpu.VMEM((NX - 1, NZ, SLAB, EXC), jnp.bfloat16),
            pltpu.VMEM((STEPS, 2, NZ, MAIN, EXC), jnp.bfloat16),
            pltpu.VMEM((STEPS + 1, OWN, EXC), jnp.float32),
            pltpu.VMEM((STEPS, OWN, EXC), jnp.float32),
            pltpu.VMEM((OWN, EXC), jnp.float32),
            pltpu.VMEM((8, NZ * NB, EXC), jnp.float32),
            pltpu.VMEM((8, NZ * NB, EXC), jnp.float32),
            pltpu.VMEM((NX - 1, NZ * NB, EXC), jnp.float32),
            pltpu.VMEM((14, NZ * NB, 16, EXC), jnp.bfloat16),
            dma, dma((STEPS, 8)), dma((STEPS, NZ, 2)), dma((STEPS, NZ, 3)), dma((STEPS, 5, 8)), dma((STEPS, 5, 2)),
            dma((STEPS, 5, 3)), dma((STEPS,)), dma((11,)),
            dma((2, 8)), dma((NZ, 2)), dma((NZ, 3)), dma((5, 7)), dma((5, 2)), dma((5, 3)), dma, dma((10,)),
        ],
        compiler_params=pltpu.CompilerParams(collective_id=0, has_side_effects=True,
                                             vmem_limit_bytes=48 * 1024 * 1024),
    )(enc, incident, pending, self_inverse, retarded)


def solution(mesh):
    in_specs = (
        P(None, "patch", None),
        P("lag", "patch", None),
        P("patch", None, None),
        P("lag", "patch", None, None, None),
        P("lag", "patch", None),
        P("lag", "patch", None),
        P(),
    )
    out_specs = (P(None, "patch", None), P("lag", "patch", None))
    return jax.shard_map(body, mesh=mesh, in_specs=in_specs, out_specs=out_specs, check_vma=False)
```

time: 162 us -> 149 us (0.920)
  the two profiles are of different devices: /device:TPU:32 before, /device:TPU:34 now
where the time goes in v2:
time: 149 us; the launch traced here: 148 us
  Pallas kernels  139 us (93%)
  local copies, waits for them, and re-layouts  6.47 us (4%)
  other arithmetic  2.32 us (2%)
    pallas_call x1, Pallas kernels, body(): pl.pallas_call(kernel, out_shape=(jax.ShapeDtypeStruct((STEPS, OWN, EXC),...  139 us
    unnamed x10, local copies, waits for them, and re-layouts  6.47 us

profile of v2, /device:TPU:34, one launch (start us, length us, event | category | flops | bytes accessed | tf_op | source)
XLA Modules:
  0.0 148.3 jit_solution(16031599071252111201)
XLA Ops:
  0.7 0.9 select_reduce_fusion
  1.5 0.7 fusion.3
  2.2 0.7 broadcast_compare_fusion
  2.9 0.1 select_reduce_fusion.1.enc
  3.0 0.0 copy-start
  3.0 2.0 %copy-done = f32[1,1,56,128,128]{4,3,2,1,0:T(8,128)S(1)} copy-done((f32[1,1,56,128,128]{4,3,2,1,0:T(8,128)S(1)}, f32[1,1,56,128,128]{4,3,2,1,0:T(8,128)}, u32[]{:S(2)}) %copy-start) | copy-done | bytes 3670040
  5.0 0.0 copy-start.1
  5.0 1.0 copy-done.1
  6.1 0.0 copy-start.2
  6.1 0.9 copy-done.2
  7.0 0.0 copy-start.3
  7.0 0.9 copy-done.3
  8.0 138.8 %shard_map.86 = (bf16[4,512,128]{2,1,0:T(8,128)(2,1)S(1)}, f32[1,512,128]{2,1,0:T(8,128)S(1)}) custom-call(s32[64]{0:T(128)S(1)} %select_reduce_fusion.1.enc, bf16[4,512,128]{2,1,0:T(8,128)(2,1)S(1)} %copy-done.1, f32[1,512,128]{2,1,0:T(8,128)S(1)} %copy-done.2, f32[4,128,128]{2,1,0:T(8,128)S(1)} %copy-done.3, f32[1,1,56,128,128]{4,3,2,1,0:T(8,128)S(1)} %copy-done), custom_call_target="tpu_custom_call" | custom-call | tf_op jit(solution)/shard_map/pallas_call | solution.py:362
  146.8 0.8 copy.11
  147.5 0.7 copy.12
Async XLA Ops:
  3.0 2.0 %copy-start = (f32[1,1,56,128,128]{4,3,2,1,0:T(8,128)S(1)}, f32[1,1,56,128,128]{4,3,2,1,0:T(8,128)}, u32[]{:S(2)}) copy-start(f32[1,1,56,128,128]{4,3,2,1,0:T(8,128)} %zmat.1) | copy-start | bytes 11010052
  5.0 1.0 copy-start.1
  6.1 0.9 copy-start.2
  7.0 0.9 copy-start.3

commit v3 on v2

--- a/solution.py
+++ b/solution.py
@@ -20,8 +20,8 @@
 MAIN, SLAB = 96, 32
 
 
-def kernel(enc, inc, pend, sinv, zmat, cur_out, ahead_out,
-           zf, w, items, slabs, pick, sbuf, pbuf, qbuf, rbuf, part, shift, acc, want, wanted, wanted2, onehot,
+def kernel(enc, inc_hbm, pend, sinv_hbm, zmat, cur_out, ahead_out,
+           inc, sinv, zf, w, items, slabs, pick, sbuf, pbuf, qbuf, rbuf, part, shift, acc, want, wanted, wanted2, onehot,
            load_sem, bc_r, z_r, s_r, x_r, r_r, p_r, sh_r, q_r,
            bc_s, z_s, s_s, x_s, r_s, p_s, sh_s, q_s):
     y = lax.axis_index("lag")
@@ -43,12 +43,16 @@
     peers = [dev(at(dz=1)), dev(at(dz=-1)), mate, dev(p, up), dev(p, down)]
     peers += [dev(at(dx=dx, core=k)) for dx in (1, 2, 3) for k in (0, 1)]
 
-    load = pltpu.make_async_copy(zmat.at[0, 0], zf, load_sem)
-    load.start()
+    loads = [pltpu.make_async_copy(pend.at[0], part.at[0], load_sem.at[0]),
+             pltpu.make_async_copy(inc_hbm, inc, load_sem.at[1]),
+             pltpu.make_async_copy(sinv_hbm, sinv, load_sem.at[2]),
+             pltpu.make_async_copy(zmat.at[0, 0], zf, load_sem.at[3])]
 
     barrier = pltpu.get_barrier_semaphore()
     for peer in peers:
         pl.semaphore_signal(barrier, inc=1, device_id=peer, device_id_type=MESH)
+    for load in loads:
+        load.start()
 
     def ask(s, carry):
         pos, t = lax.div(s, 8), lax.rem(s, 8)
@@ -58,7 +62,8 @@
         return carry
 
     lax.fori_loop(0, 64, ask, 0)
-    part[0] = pend[0]
+    for load in loads[:3]:
+        load.wait()
     pl.semaphore_wait(barrier, len(peers))
 
     def remote(src, dst, ssem, rsem, where):
@@ -91,8 +96,7 @@
             return remote(piece, piece, bc_s.at[sem, i], bc_r.at[n, i], dev(p, lag))
 
         def ring(d_from, d_to, k, dz):
-            half = pl.ds(2 * k, 2)
-            return remote(items.at[n, d_from, half], items.at[n, d_to, half], z_s.at[d_to, k],
+            return remote(items.at[n, d_from, k], items.at[n, d_to, k], z_s.at[d_to, k],
                           z_r.at[n, d_to, k], dev(at(dz=dz)))
 
         def slab_start():
@@ -203,9 +207,9 @@
             pl.when(y != 0)(arrives(piece, bc_r.at[n, i]))
             pl.when(goes_up[i // 4])(bcast(i, up, 0).start)
             pl.when(goes_down[i // 4])(bcast(i, down, 1).start)
-            if i % 4 == 3:
-                ring(0, 1, i // 4, 1).start()
-                ring(0, 7, i // 4, -1).start()
+            if i % 2 == 1:
+                ring(0, 1, i // 2, 1).start()
+                ring(0, 7, i // 2, -1).start()
         for copy in slab_start():
             copy.start()
 
@@ -242,42 +246,41 @@
         move = remote(part.at[n], shift.at[n], sh_s, sh_r.at[n], dev(p, down))
         pl.when(y != 0)(move.start)
 
-        def hop(make, a, b, arrive):
-            for k in range(2):
-                make(a[0] - 1, a[0], k, 1).wait_recv()
-                if arrive == 3:
-                    if k == 0:
-                        make(a[0], 4, 0, 1).start()
-                else:
-                    make(a[0], a[0] + 1, k, 1).start()
-                make(b[0], b[0], k, -1).wait_recv()
-                if arrive == 3:
-                    if k == 1:
-                        make(b[0], 4, 1, -1).start()
-                else:
-                    make(b[0], b[0] - 1, k, -1).start()
-
-        hop(ring, (1,), (7,), 1)
+        def hop(make, pieces, h):
+            for k in range(pieces):
+                below = 2 * k < pieces
+                make(h - 1, h, k, 1).wait_recv()
+                if h < 3 or below:
+                    make(h, h + 1, k, 1).start()
+                make((9 - h) % 8, 8 - h, k, -1).wait_recv()
+                if h < 3 or not below:
+                    make(8 - h, 7 - h, k, -1).start()
+
+        def last(make, pieces):
+            for k in range(pieces):
+                (make(3, 4, k, 1) if 2 * k < pieces else make(5, 4, k, -1)).wait_recv()
+
+        hop(ring, 4, 1)
+        pass_on(1)
         for i in range(3):
             arrives(slabs.at[n, 0, i], s_r.at[n, 0, i])()
         for k in range(2):
             slab_ring(0, 1, k, 1).start()
             slab_ring(0, 7, k, -1).start()
-        pass_on(1)
-        hop(ring, (2,), (6,), 2)
+        hop(ring, 4, 2)
+        pass_on(2)
         relay(0)
-        hop(slab_ring, (1,), (7,), 1)
-        pass_on(2)
+        hop(slab_ring, 2, 1)
         slab_pass(0)
-        hop(ring, (3,), (5,), 3)
+        hop(ring, 4, 3)
+        pass_on(3)
         relay(1)
-        pass_on(3)
-        hop(slab_ring, (2,), (6,), 2)
+        hop(slab_ring, 2, 2)
         slab_pass(1)
 
         @pl.when(first)
         def _():
-            pltpu.make_async_copy(zmat.at[0, 0], zf, load_sem).wait()
+            loads[3].wait()
 
             def place(s, carry):
                 code = enc[s]
@@ -291,23 +294,20 @@
 
             lax.fori_loop(0, 64, place, 0)
 
+        last(ring, 4)
+        pass_on(4)
         relay(2)
-        ring(3, 4, 0, 1).wait_recv()
-        ring(5, 4, 1, -1).wait_recv()
-        pass_on(4)
         apply(0)
-        hop(slab_ring, (3,), (5,), 3)
+        hop(slab_ring, 2, 3)
         slab_pass(2)
         relay(3)
         apply(1)
+        last(slab_ring, 2)
         slab_pass(3)
+        slab_pass(4)
         relay(4)
-        apply(2)
-        slab_ring(3, 4, 0, 1).wait_recv()
-        slab_ring(5, 4, 1, -1).wait_recv()
-        slab_pass(4)
-        apply(3)
-        apply(4)
+        for g in range(2, 5):
+            apply(g)
 
         pl.when(y != NY - 1)(move.wait_recv)
 
@@ -322,12 +322,12 @@
         for i in range(8):
             pl.when(goes_up[i // 4])(bcast(i, up, 0).wait_send)
             pl.when(goes_down[i // 4])(bcast(i, down, 1).wait_send)
-        for make in (ring, slab_ring):
-            for k in range(2):
-                for d_from, d_to, dz in ((0, 1, 1), (1, 2, 1), (2, 3, 1), (0, 7, -1), (7, 6, -1), (6, 5, -1)):
-                    make(d_from, d_to, k, dz).wait_send()
-            make(3, 4, 0, 1).wait_send()
-            make(5, 4, 1, -1).wait_send()
+        for make, pieces in ((ring, 4), (slab_ring, 2)):
+            for k in range(pieces):
+                for h in range(3):
+                    make(h, h + 1, k, 1).wait_send()
+                    make((8 - h) % 8, 7 - h, k, -1).wait_send()
+                (make(3, 4, k, 1) if 2 * k < pieces else make(5, 4, k, -1)).wait_send()
         for copy in slab_start():
             copy.wait_send()
         for g in range(5):
@@ -358,15 +358,17 @@
     hit = (slot[None, :] == jnp.arange(64)[:, None]) & live[None, :]
     enc = jnp.max(jnp.where(hit, code[None, :], -1), axis=1).astype(jnp.int32)
     vmem = pl.BlockSpec(memory_space=pltpu.VMEM)
+    hbm = pl.BlockSpec(memory_space=pltpu.HBM)
     dma = pltpu.SemaphoreType.DMA
     return pl.pallas_call(
         kernel,
         out_shape=(jax.ShapeDtypeStruct((STEPS, OWN, EXC), jnp.bfloat16),
                    jax.ShapeDtypeStruct((1, OWN, EXC), jnp.float32)),
-        in_specs=[pl.BlockSpec(memory_space=pltpu.SMEM), vmem, vmem, vmem,
-                  pl.BlockSpec(memory_space=pl.ANY)],
+        in_specs=[pl.BlockSpec(memory_space=pltpu.SMEM), hbm, hbm, hbm, hbm],
         out_specs=(vmem, vmem),
         scratch_shapes=[
+            pltpu.VMEM((STEPS, OWN, EXC), jnp.bfloat16),
+            pltpu.VMEM((NB, B, B), jnp.float32),
             pltpu.VMEM((LIST, B, B), jnp.float32),
             pltpu.VMEM((NZ, OWN, 8 * B), jnp.bfloat16),
             pltpu.VMEM((STEPS, NZ, NB, B, EXC), jnp.bfloat16),
@@ -383,13 +385,13 @@
             pltpu.VMEM((8, NZ * NB, EXC), jnp.float32),
             pltpu.VMEM((NX - 1, NZ * NB, EXC), jnp.float32),
             pltpu.VMEM((14, NZ * NB, 16, EXC), jnp.bfloat16),
-            dma, dma((STEPS, 8)), dma((STEPS, NZ, 2)), dma((STEPS, NZ, 3)), dma((STEPS, 5, 8)), dma((STEPS, 5, 2)),
+            dma((4,)), dma((STEPS, 8)), dma((STEPS, NZ, 4)), dma((STEPS, NZ, 3)), dma((STEPS, 5, 8)), dma((STEPS, 5, 2)),
             dma((STEPS, 5, 3)), dma((STEPS,)), dma((11,)),
-            dma((2, 8)), dma((NZ, 2)), dma((NZ, 3)), dma((5, 7)), dma((5, 2)), dma((5, 3)), dma, dma((10,)),
+            dma((2, 8)), dma((NZ, 4)), dma((NZ, 3)), dma((5, 7)), dma((5, 2)), dma((5, 3)), dma, dma((10,)),
         ],
         compiler_params=pltpu.CompilerParams(collective_id=0, has_side_effects=True,
                                              vmem_limit_bytes=48 * 1024 * 1024),
-    )(enc, incident, pending, self_inverse, retarded)
+    )(enc, *(pltpu.with_memory_space_constraint(a, pltpu.HBM) for a in (incident, pending, self_inverse, retarded)))
 
 
 def solution(mesh):

time: 149 us -> 145 us (0.973)
  the two profiles are of different devices: /device:TPU:34 before, /device:TPU:32 now
where the time goes in v3:
time: 145 us; the launch traced here: 144 us
  Pallas kernels  140 us (97%)
  other arithmetic  2.32 us (2%)
  local copies, waits for them, and re-layouts  1.5 us (1%)
    pallas_call x1, Pallas kernels, body(): pl.pallas_call(kernel, out_shape=(jax.ShapeDtypeStruct((STEPS, OWN, EXC),...  140 us

profile of v3, /device:TPU:32, one launch (start us, length us, event | category | flops | bytes accessed | tf_op | source)
XLA Modules:
  0.0 144.5 jit_solution(480031573156494646)
XLA Ops:
  0.7 0.9 select_reduce_fusion
  1.5 0.7 fusion.3
  2.2 0.7 broadcast_compare_fusion
  2.9 0.1 select_reduce_fusion.1.enc
  3.0 140.0 %shard_map.86 = (bf16[4,512,128]{2,1,0:T(8,128)(2,1)S(1)}, f32[1,512,128]{2,1,0:T(8,128)S(1)}) custom-call(s32[64]{0:T(128)S(1)} %select_reduce_fusion.1.enc, bf16[4,512,128]{2,1,0:T(8,128)(2,1)} %inc_hbm.1, f32[1,512,128]{2,1,0:T(8,128)} %pend.1, f32[4,128,128]{2,1,0:T(8,128)} %sinv_hbm.1, f32[1,1,56,128,128]{4,3,2,1,0:T(8,128)} %zmat.1), custom_call_target="tpu_custom_call" | custom-call | tf_op jit(solution)/shard_map/pallas_call | solution.py:363
  143.0 0.8 copy.11
  143.8 0.7 copy.12

commit v4 on v3

v4 whole, which is shorter than its diff:
```python
import jax
import jax.numpy as jnp
from jax import lax
from jax.experimental import pallas as pl
from jax.experimental.pallas import tpu as pltpu
from jax.sharding import PartitionSpec as P

EXC = 128
B = 128
NB = 4
OWN = NB * B
STEPS = 4
LIST = 56
SRC = 256
NX, NZ, NY = 4, 8, 8
MESH = pl.DeviceIdType.MESH

ORDER = (0, 1, 7, 2, 6, 3, 5, 4)
GROUPS = ((0, 1), (1, 3), (3, 5), (5, 7), (7, 8))
HALF = B // 2
MAIN, SLAB = 48, 16


def kernel(enc, inc_hbm, pend_hbm, sinv_hbm, zmat, cur_out, ahead_out,
           inc, pend, sinv, zf, w, items, slabs, pick, sbuf, pbuf, qbuf, rbuf, part, shift, acc, want, wanted, wanted2, onehot,
           load_sem, bc_r, z_r, s_r, x_r, r_r, p_r, sh_r, q_r,
           bc_s, z_s, s_s, x_s, r_s, p_s, sh_s, q_s):
    y = lax.axis_index("lag")
    p = lax.axis_index("patch")
    c = lax.rem(p, 2)
    x = lax.rem(lax.div(p, 2), NX)
    z = lax.div(p, 2 * NX)

    def at(dx=0, dz=0, core=None):
        core = c if core is None else core
        return lax.rem(z + dz + NZ, NZ) * (2 * NX) + lax.rem(x + dx, NX) * 2 + core

    def dev(patch, lag=None):
        return {"lag": y if lag is None else lag, "patch": patch}

    up, down = lax.rem(y + 1, NY), lax.rem(y + NY - 1, NY)
    partner = 1 - c
    mate = dev(at(core=partner))
    peers = [dev(at(dz=1)), dev(at(dz=-1)), mate, dev(p, up), dev(p, down)]
    peers += [dev(at(dx=dx, core=k)) for dx in (1, 2, 3) for k in (0, 1)]

    loads = [pltpu.make_async_copy(pend_hbm.at[0], pend, load_sem.at[0]),
             pltpu.make_async_copy(inc_hbm, inc, load_sem.at[1]),
             pltpu.make_async_copy(sinv_hbm, sinv, load_sem.at[2]),
             pltpu.make_async_copy(zmat.at[0, 0], zf, load_sem.at[3])]

    barrier = pltpu.get_barrier_semaphore()
    for peer in peers:
        pl.semaphore_signal(barrier, inc=1, device_id=peer, device_id_type=MESH)
    for load in loads:
        load.start()

    def ask(s, carry):
        pos, t = lax.div(s, 8), lax.rem(s, 8)
        local = jnp.maximum(enc[s], 0) & 3
        for k in range(NB):
            want[t, pl.ds(pos * NB + k, 1), :] = jnp.full((1, EXC), jnp.where(local == k, 1.0, 0.0), jnp.float32)
        return carry

    lax.fori_loop(0, 64, ask, 0)
    for load in loads[:3]:
        load.wait()
    low = lax.broadcasted_iota(jnp.int32, (OWN // 2, EXC), 1) < HALF
    low_b = low[:B]
    low_h = low[:HALF]

    def roll(v):
        return pltpu.roll(v, HALF, 1)

    top, bottom = pend[: OWN // 2], pend[OWN // 2 :]
    part[0, 0] = jnp.where(low, top, roll(bottom))
    part[1, 0] = jnp.where(low, roll(top), bottom)
    pl.semaphore_wait(barrier, len(peers))

    def remote(src, dst, ssem, rsem, where):
        return pltpu.make_async_remote_copy(
            src_ref=src, dst_ref=dst, send_sem=ssem, recv_sem=rsem,
            device_id=where, device_id_type=MESH)

    def arrives(ref, rsem):
        return remote(ref, ref, sh_s.at[0], rsem, mate).wait_recv

    def asks():
        out = [remote(want.at[partner], wanted.at[c], q_s.at[0], q_r.at[c], mate)]
        for dx in (1, 2, 3):
            out.append(remote(want.at[dx * 2 + partner], wanted2.at[dx - 1], q_s.at[6 + dx], q_r.at[7 + dx], mate))
            for k in (0, 1):
                t, back = dx * 2 + k, (NX - dx) * 2
                out.append(remote(want.at[t], wanted.at[back + c], q_s.at[t - 1], q_r.at[back + c],
                                  dev(at(dx=dx, core=k))))
        return out

    for copy in asks():
        copy.start()

    def chain(n, h):
        def bcast(i, lag, sem):
            piece = items.at[n, h, 0, i]
            return remote(piece, piece, bc_s.at[h, sem, i], bc_r.at[n, h, i], dev(p, lag))

        def ring(d_from, d_to, k, dz):
            half = pl.ds(2 * k, 2)
            return remote(items.at[n, h, d_from, half], items.at[n, h, d_to, half], z_s.at[h, d_to, k],
                          z_r.at[n, h, d_to, k], dev(at(dz=dz)))

        def slab_start():
            return [remote(items.at[n, h, 0, :, pl.ds(MAIN, SLAB)], slabs.at[n, h, 0, NX - dx - 1],
                           s_s.at[h, 0, dx - 1], s_r.at[n, h, 0, NX - dx - 1], dev(at(dx=dx))) for dx in (2, 1, 3)]

        def slab_ring(d_from, d_to, k, dz):
            half = pl.ds(2 * k, 2)
            return remote(slabs.at[n, h, d_from, :, half], slabs.at[n, h, d_to, :, half], s_s.at[h, d_to, k],
                          s_r.at[n, h, d_to, k], dev(at(dz=dz)))

        def span_of(g):
            p0, p1 = GROUPS[g]
            return pl.ds(p0, p1 - p0)

        def rows_of(slot, offset, size):
            return pl.ds(pl.multiple_of(slot * HALF + offset, 16), size)

        def sends(g):
            span = span_of(g)
            out = []
            for k, dx in ((0, 1), (1, 3)):
                out.append(remote(sbuf.at[h, 2 + k, span], rbuf.at[n, h, k, span], x_s.at[h, g, 3 + k],
                                  r_r.at[n, h, g, k], dev(at(dx=dx))))
            for dx in (1, 3):
                for k in (0, 1):
                    t, back = dx * 2 + k, (NX - dx) * 2 + c
                    out.append(remote(
                        sbuf.at[h, t - 2, span], pick.at[n, h, span, rows_of(back, 0, MAIN)],
                        x_s.at[h, g, t - 1], x_r.at[n, h, g, back], dev(at(dx=dx, core=k))))
            out.append(remote(pbuf.at[h, span], pick.at[n, h, span, rows_of(c, 0, HALF)], x_s.at[h, g, 0],
                              x_r.at[n, h, g, c], mate))
            return out

        def slab_sends(g):
            span = span_of(g)
            return [remote(qbuf.at[h, dx - 1, span], pick.at[n, h, span, rows_of(dx * 2 + c, MAIN, SLAB)],
                           p_s.at[h, g, dx - 1], p_r.at[n, h, g, dx - 1], mate) for dx in (1, 2, 3)]

        def relays(g):
            span = span_of(g)
            return [remote(rbuf.at[n, h, k, span], pick.at[n, h, span, rows_of(4 + c, 0, MAIN)], r_s.at[h, g, k],
                           x_r.at[n, h, g, 4 + c], dev(at(dx=dx, core=k))) for k, dx in ((0, 1), (1, 3))]

        def choose(blocks, table, pos, rows):
            total = None
            for k in range(NB):
                term = blocks[k].reshape(rows // 16, 16, EXC) * onehot[table, pos * NB + k][None]
                total = term if total is None else total + term
            return total.reshape(rows, EXC)

        def pass_on(g):
            for pos in range(*GROUPS[g]):
                whole = [items[n, h, ORDER[pos], k] for k in range(NB)]
                head = [block[:MAIN] for block in whole]
                for t in (4, 5, 2, 3, 6, 7):
                    sbuf[h, t - 2, pos] = choose(head, t, pos, MAIN)
                pbuf[h, pos] = choose(whole, partner, pos, HALF)
                pick[n, h, pos, rows_of(c, 0, HALF), :] = choose(whole, c, pos, HALF)
            for copy in sends(g):
                copy.start()

        def slab_pass(g):
            for pos in range(*GROUPS[g]):
                for dx in (1, 2, 3):
                    blocks = [slabs[n, h, ORDER[pos], dx - 1, k] for k in range(NB)]
                    qbuf[h, dx - 1, pos] = choose(blocks, 11 + dx - 1, pos, SLAB)
                    pick[n, h, pos, rows_of(dx * 2 + c, MAIN, SLAB), :] = choose(blocks, 8 + dx - 1, pos, SLAB)
            for copy in slab_sends(g):
                copy.start()

        def relay(g):
            for k, copy in enumerate(relays(g)):
                arrives(rbuf.at[n, h, k, span_of(g)], r_r.at[n, h, g, k])()
                copy.start()

        def apply(g):
            span = span_of(g)
            for s in range(8):
                if s < 2:
                    pl.when(c != s)(arrives(pick.at[n, h, span, pl.ds(s * HALF, HALF)], x_r.at[n, h, g, s]))
                else:
                    arrives(pick.at[n, h, span, pl.ds(s * HALF, MAIN)], x_r.at[n, h, g, s])()
            for dx in (1, 2, 3):
                arrives(pick.at[n, h, span, rows_of(dx * 2 + partner, MAIN, SLAB)], p_r.at[n, h, g, dx - 1])()
            for pos in range(*GROUPS[g]):
                term = jnp.dot(w[pos], pick[n, h, pos], preferred_element_type=jnp.float32)
                if pos == 0:
                    acc[h] = term
                else:
                    acc[h] += term

        def hop(make, i):
            for k in range(2):
                make(i - 1, i, k, 1).wait_recv()
                if i < 3 or k == 0:
                    make(i, i + 1, k, 1).start()
                make((9 - i) % 8, 8 - i, k, -1).wait_recv()
                if i < 3 or k == 1:
                    make(8 - i, 7 - i, k, -1).start()

        def last(make):
            make(3, 4, 0, 1).wait_recv()
            make(5, 4, 1, -1).wait_recv()

        move = remote(part.at[h, n], shift.at[h, n], sh_s.at[h], sh_r.at[n, h], dev(p, down))
        goes_up = [y <= 3, y <= 2]
        goes_down = [(y == 0) | (y >= 6), (y == 0) | (y >= 5)]

        def begin():
            @pl.when(y == 0)
            def _():
                for j in range(2):
                    rows = pl.ds(j * B, B)
                    left, right = inc[n, rows].astype(jnp.float32), inc[n, pl.ds(2 * B + j * B, B)].astype(jnp.float32)
                    if h == 0:
                        due = jnp.where(low_b, left, roll(right))
                    else:
                        due = jnp.where(low_b, roll(left), right)
                    excess = due - part[h, n, rows]
                    for k in (j, j + 2):
                        solved = jnp.dot(sinv[k], excess, precision=lax.Precision.HIGHEST,
                                         preferred_element_type=jnp.float32)
                        first_rows, last_rows = solved[:HALF], solved[HALF:]
                        if k == j:
                            packed = jnp.where(low_h, first_rows, roll(last_rows))
                        else:
                            packed = jnp.where(low_h, roll(first_rows), last_rows)
                        items[n, h, 0, k] = packed.astype(jnp.bfloat16)

            for i in range(NB):
                pl.when(y != 0)(arrives(items.at[n, h, 0, i], bc_r.at[n, h, i]))
                pl.when(goes_up[i // 2])(bcast(i, up, 0).start)
                pl.when(goes_down[i // 2])(bcast(i, down, 1).start)
                if i % 2 == 1:
                    ring(0, 1, i // 2, 1).start()
                    ring(0, 7, i // 2, -1).start()
            for copy in slab_start():
                copy.start()
            if h == 0:
                pl.when(n == 0)(tables)
            pass_on(0)
            pl.when(y != 0)(move.start)
            if h == 1:
                for k in range(NB):
                    a, b = items[n, 0, 0, k].astype(jnp.float32), items[n, 1, 0, k].astype(jnp.float32)
                    cur_out[n, pl.ds(k * B, HALF)] = jnp.where(low_h, a, roll(b)).astype(jnp.bfloat16)
                    cur_out[n, pl.ds(k * B + HALF, HALF)] = jnp.where(low_h, roll(a), b).astype(jnp.bfloat16)

        def stage1():
            hop(ring, 1)
            pass_on(1)
            for i in range(3):
                arrives(slabs.at[n, h, 0, i], s_r.at[n, h, 0, i])()
            for k in range(2):
                slab_ring(0, 1, k, 1).start()
                slab_ring(0, 7, k, -1).start()

        def stage2():
            hop(ring, 2)
            pass_on(2)
            relay(0)

        def stage3():
            hop(slab_ring, 1)
            slab_pass(0)
            hop(ring, 3)
            pass_on(3)
            relay(1)

        def stage4():
            hop(slab_ring, 2)
            slab_pass(1)
            last(ring)
            pass_on(4)
            relay(2)
            if h == 0:
                pl.when(n == 0)(operator)

        def stage5():
            apply(0)
            hop(slab_ring, 3)
            slab_pass(2)
            relay(3)

        def stage6():
            apply(1)
            apply(2)
            last(slab_ring)
            slab_pass(3)
            slab_pass(4)
            relay(4)

        def finish():
            apply(3)
            apply(4)
            fresh = acc[h, pl.ds(0, OWN)] + roll(acc[h, pl.ds(OWN, OWN)])
            packed = jnp.where(low, fresh[: OWN // 2], roll(fresh[OWN // 2 :]))
            pl.when(y != NY - 1)(move.wait_recv)

            @pl.when(y != NY - 1)
            def _():
                part[h, n + 1] = packed + shift[h, n]

            @pl.when(y == NY - 1)
            def _():
                part[h, n + 1] = packed

            for i in range(NB):
                pl.when(goes_up[i // 2])(bcast(i, up, 0).wait_send)
                pl.when(goes_down[i // 2])(bcast(i, down, 1).wait_send)
            for make in (ring, slab_ring):
                for k in range(2):
                    for i in range(3):
                        make(i, i + 1, k, 1).wait_send()
                        make((8 - i) % 8, 7 - i, k, -1).wait_send()
                make(3, 4, 0, 1).wait_send()
                make(5, 4, 1, -1).wait_send()
            for copy in slab_start():
                copy.wait_send()
            for g in range(5):
                for copy in sends(g) + relays(g) + slab_sends(g):
                    copy.wait_send()
            pl.when(y != 0)(move.wait_send)

        return [begin, stage1, stage2, stage3, stage4, stage5, stage6, finish]

    def tables():
        for t in range(8):
            if t < 2:
                pl.when(c != t)(arrives(wanted.at[t], q_r.at[t]))
            else:
                arrives(wanted.at[t], q_r.at[t])()
        wanted[c] = want[c]
        for dx in (1, 2, 3):
            arrives(wanted2.at[dx - 1], q_r.at[7 + dx])()

        def line(rows):
            return jnp.broadcast_to(rows, (16, EXC)).astype(jnp.bfloat16)

        def spread(t, carry):
            for r in range(NB * NZ):
                onehot[t, r] = line(wanted[t, pl.ds(r, 1), :])
            return carry

        def spread_slabs(i, carry):
            for r in range(NB * NZ):
                onehot[8 + i, r] = line(want[i * 2 + 2 + c, pl.ds(r, 1), :])
                onehot[11 + i, r] = line(wanted2[i, pl.ds(r, 1), :])
            return carry

        lax.fori_loop(0, 8, spread, 0)
        lax.fori_loop(0, 3, spread_slabs, 0)

    def operator():
        loads[3].wait()

        def place(pair, carry):
            pos, col = lax.div(pair, 4), lax.rem(pair, 4)
            codes = [enc[2 * pair], enc[2 * pair + 1]]
            rows = [jnp.where(code < 0, -1, (code >> 2) & 3) for code in codes]
            even, odd = [zf[jnp.maximum(code, 0) >> 4] for code in codes]
            even_turned, odd_turned = roll(even), roll(odd)
            lanes = pl.ds(pl.multiple_of(col * B, B), B)
            for r in range(NB):
                keep = [jnp.where(row == r, 1.0, 0.0) for row in rows]
                w[pos, pl.ds(r * B, B), lanes] = jnp.where(
                    low_b, even * keep[0], odd_turned * keep[1]).astype(jnp.bfloat16)
                w[pos, pl.ds(OWN + r * B, B), lanes] = jnp.where(
                    low_b, even_turned * keep[0], odd * keep[1]).astype(jnp.bfloat16)
            return carry

        lax.fori_loop(0, 32, place, 0)

    def step(n, carry):
        ahead, behind, late = chain(n, 0), chain(n, 1), chain(n - 1, 1)
        for i in range(4):
            pl.when(n < STEPS)(ahead[i])
            pl.when(n > 0)(late[i + 4])
        for i in range(4):
            pl.when(n < STEPS)(ahead[i + 4])
            pl.when(n < STEPS)(behind[i])
        return carry

    lax.fori_loop(0, STEPS + 1, step, 0)
    for copy in asks():
        copy.wait_send()
    a, b = part[0, STEPS], part[1, STEPS]
    ahead_out[0, pl.ds(0, OWN // 2)] = jnp.where(low, a, roll(b))
    ahead_out[0, pl.ds(OWN // 2, OWN // 2)] = jnp.where(low, roll(a), b)


def body(incident, pending, self_inverse, retarded, block_rows, block_sources, owner_map):
    p = lax.axis_index("patch")
    x, z = (p // 2) % NX, p // (2 * NX)
    row = block_rows[0, 0]
    source = block_sources[0, 0]
    live = source >= 0
    storage = jnp.sum(jnp.where(source[:, None] == jnp.arange(SRC)[None, :], owner_map[None, :], 0), axis=1)
    owner, local = storage // NB, storage % NB
    d = (z - owner // (2 * NX)) % NZ
    pos = jnp.where(d == 0, 0, jnp.where(d <= 3, 2 * d - 1, jnp.where(d == 4, 7, 2 * (NZ - d))))
    column = ((owner // 2) % NX - x) % NX * 2 + owner % 2
    slot = pos * 8 + column
    code = jnp.arange(LIST, dtype=jnp.int32) * 16 + row * 4 + local
    hit = (slot[None, :] == jnp.arange(64)[:, None]) & live[None, :]
    enc = jnp.max(jnp.where(hit, code[None, :], -1), axis=1).astype(jnp.int32)
    vmem = pl.BlockSpec(memory_space=pltpu.VMEM)
    hbm = pl.BlockSpec(memory_space=pltpu.HBM)
    dma = pltpu.SemaphoreType.DMA
    return pl.pallas_call(
        kernel,
        out_shape=(jax.ShapeDtypeStruct((STEPS, OWN, EXC), jnp.bfloat16),
                   jax.ShapeDtypeStruct((1, OWN, EXC), jnp.float32)),
        in_specs=[pl.BlockSpec(memory_space=pltpu.SMEM), hbm, hbm, hbm, hbm],
        out_specs=(vmem, vmem),
        scratch_shapes=[
            pltpu.VMEM((STEPS, OWN, EXC), jnp.bfloat16),
            pltpu.VMEM((OWN, EXC), jnp.float32),
            pltpu.VMEM((NB, B, B), jnp.float32),
            pltpu.VMEM((LIST, B, B), jnp.float32),
            pltpu.VMEM((NZ, 2 * OWN, 8 * HALF), jnp.bfloat16),
            pltpu.VMEM((STEPS, 2, NZ, NB, HALF, EXC), jnp.bfloat16),
            pltpu.VMEM((STEPS, 2, NZ, NX - 1, NB, SLAB, EXC), jnp.bfloat16),
            pltpu.VMEM((STEPS, 2, NZ, 8 * HALF, EXC), jnp.bfloat16),
            pltpu.VMEM((2, 6, NZ, MAIN, EXC), jnp.bfloat16),
            pltpu.VMEM((2, NZ, HALF, EXC), jnp.bfloat16),
            pltpu.VMEM((2, NX - 1, NZ, SLAB, EXC), jnp.bfloat16),
            pltpu.VMEM((STEPS, 2, 2, NZ, MAIN, EXC), jnp.bfloat16),
            pltpu.VMEM((2, STEPS + 1, OWN // 2, EXC), jnp.float32),
            pltpu.VMEM((2, STEPS, OWN // 2, EXC), jnp.float32),
            pltpu.VMEM((2, 2 * OWN, EXC), jnp.float32),
            pltpu.VMEM((8, NZ * NB, EXC), jnp.float32),
            pltpu.VMEM((8, NZ * NB, EXC), jnp.float32),
            pltpu.VMEM((NX - 1, NZ * NB, EXC), jnp.float32),
            pltpu.VMEM((14, NZ * NB, 16, EXC), jnp.bfloat16),
            dma((4,)), dma((STEPS, 2, NB)), dma((STEPS, 2, NZ, 2)), dma((STEPS, 2, NZ, 3)), dma((STEPS, 2, 5, 8)),
            dma((STEPS, 2, 5, 2)), dma((STEPS, 2, 5, 3)), dma((STEPS, 2)), dma((11,)),
            dma((2, 2, NB)), dma((2, NZ, 2)), dma((2, NZ, 3)), dma((2, 5, 7)), dma((2, 5, 2)), dma((2, 5, 3)),
            dma((2,)), dma((10,)),
        ],
        compiler_params=pltpu.CompilerParams(collective_id=0, has_side_effects=True,
                                             vmem_limit_bytes=48 * 1024 * 1024),
    )(enc, *(pltpu.with_memory_space_constraint(a, pltpu.HBM) for a in (incident, pending, self_inverse, retarded)))


def solution(mesh):
    in_specs = (
        P(None, "patch", None),
        P("lag", "patch", None),
        P("patch", None, None),
        P("lag", "patch", None, None, None),
        P("lag", "patch", None),
        P("lag", "patch", None),
        P(),
    )
    out_specs = (P(None, "patch", None), P("lag", "patch", None))
    return jax.shard_map(body, mesh=mesh, in_specs=in_specs, out_specs=out_specs, check_vma=False)
```

time: 145 us -> 165 us (1.14)
  Pallas kernels: 140 us -> 161 us
    pallas_call x1, Pallas kernels: 140 us -> 161 us  [body(): pl.pallas_call(kernel, out_shape=(jax.ShapeDtypeStruct((STEPS, OWN, EXC),...]
where the time goes in v4:
time: 165 us
  Pallas kernels  161 us (98%)
  other arithmetic  2.32 us (1%)
    pallas_call x1, Pallas kernels, body(): pl.pallas_call(kernel, out_shape=(jax.ShapeDtypeStruct((STEPS, OWN, EXC),...  161 us

profile of v4, /device:TPU:32, one launch (start us, length us, event | category | flops | bytes accessed | tf_op | source)
XLA Modules:
  0.0 165.3 jit_solution(8644240117586255515)
XLA Ops:
  0.7 0.9 select_reduce_fusion
  1.5 0.7 fusion.3
  2.2 0.7 broadcast_compare_fusion
  2.9 0.1 select_reduce_fusion.1.enc
  3.0 160.8 %shard_map.86 = (bf16[4,512,128]{2,1,0:T(8,128)(2,1)S(1)}, f32[1,512,128]{2,1,0:T(8,128)S(1)}) custom-call(s32[64]{0:T(128)S(1)} %select_reduce_fusion.1.enc, bf16[4,512,128]{2,1,0:T(8,128)(2,1)} %inc_hbm.1, f32[1,512,128]{2,1,0:T(8,128)} %pend_hbm.1, f32[4,128,128]{2,1,0:T(8,128)} %sinv_hbm.1, f32[1,1,56,128,128]{4,3,2,1,0:T(8,128)} %zmat.1), custom_call_target="tpu_custom_call" | custom-call | tf_op jit(solution)/shard_map/pallas_call | solution.py:419
  163.8 0.8 copy.11
  164.6 0.7 copy.12

commit v5 on v3

--- a/solution.py
+++ b/solution.py
@@ -21,9 +21,9 @@
 
 
 def kernel(enc, inc_hbm, pend, sinv_hbm, zmat, cur_out, ahead_out,
-           inc, sinv, zf, w, items, slabs, pick, sbuf, pbuf, qbuf, rbuf, part, shift, acc, want, wanted, wanted2, onehot,
-           load_sem, bc_r, z_r, s_r, x_r, r_r, p_r, sh_r, q_r,
-           bc_s, z_s, s_s, x_s, r_s, p_s, sh_s, q_s):
+           inc, sinv, zf, w, items, slabs, pick, sbuf, pbuf, qbuf, part, shift, acc, want, wanted, wanted2, onehot,
+           load_sem, bc_r, z_r, s_r, x_r, p_r, sh_r, q_r,
+           bc_s, z_s, s_s, x_s, p_s, sh_s, q_s):
     y = lax.axis_index("lag")
     p = lax.axis_index("patch")
     c = lax.rem(p, 2)
@@ -38,9 +38,10 @@
         return {"lag": y if lag is None else lag, "patch": patch}
 
     up, down = lax.rem(y + 1, NY), lax.rem(y + NY - 1, NY)
+    up2, down2 = lax.rem(y + 2, NY), lax.rem(y + NY - 2, NY)
     partner = 1 - c
     mate = dev(at(core=partner))
-    peers = [dev(at(dz=1)), dev(at(dz=-1)), mate, dev(p, up), dev(p, down)]
+    peers = [dev(at(dz=1)), dev(at(dz=-1)), mate, dev(p, up), dev(p, down), dev(p, up2), dev(p, down2)]
     peers += [dev(at(dx=dx, core=k)) for dx in (1, 2, 3) for k in (0, 1)]
 
     loads = [pltpu.make_async_copy(pend.at[0], part.at[0], load_sem.at[0]),
@@ -62,8 +63,20 @@
         return carry
 
     lax.fori_loop(0, 64, ask, 0)
-    for load in loads[:3]:
+    for load in loads:
         load.wait()
+
+    def place(s, carry):
+        code = enc[s]
+        row = jnp.where(code < 0, -1, (code >> 2) & 3)
+        block = zf[jnp.maximum(code, 0) >> 4].astype(jnp.bfloat16)
+        pos, col = lax.div(s, 8), lax.rem(s, 8)
+        for r in range(NB):
+            keep = jnp.where(row == r, 1.0, 0.0).astype(jnp.bfloat16)
+            w[pos, pl.ds(r * B, B), pl.ds(pl.multiple_of(col * B, B), B)] = block * keep
+        return carry
+
+    lax.fori_loop(0, 64, place, 0)
     pl.semaphore_wait(barrier, len(peers))
 
     def remote(src, dst, ssem, rsem, where):
@@ -91,9 +104,14 @@
         def mine(row):
             return pl.ds(pl.multiple_of(row * B, B), B)
 
-        def bcast(i, lag, sem):
-            piece = items.at[n, 0, i // 2, pl.ds((i % 2) * (B // 2), B // 2)]
-            return remote(piece, piece, bc_s.at[sem, i], bc_r.at[n, i], dev(p, lag))
+        def piece(i):
+            return items.at[n, 0, i // 2, pl.ds((i % 2) * (B // 2), B // 2)]
+
+        def bcast(i, way):
+            lag = (up2, down2, up, down)[way]
+            goes = ((y == 0) | ((y == 2) & (i < 4)), (y == 0) | ((y == 6) & (i >= 4)),
+                    (y == 0) | (y == 2), (y == 0) | (y == 6))[way]
+            return goes, remote(piece(i), piece(i), bc_s.at[way, i], bc_r.at[n, i], dev(p, lag))
 
         def ring(d_from, d_to, k, dz):
             return remote(items.at[n, d_from, k], items.at[n, d_to, k], z_s.at[d_to, k],
@@ -115,9 +133,10 @@
         def sends(g):
             span = span_of(g)
             out = []
-            for k, dx in ((0, 1), (1, 3)):
-                out.append(remote(sbuf.at[2 + k, span], rbuf.at[n, k, span], x_s.at[g, 3 + k],
-                                  r_r.at[n, g, k], dev(at(dx=dx))))
+            for k in (0, 1):
+                out.append(remote(sbuf.at[2 + k, span],
+                                  pick.at[n, span, pl.ds(pl.multiple_of((4 + c) * B, B), MAIN)],
+                                  x_s.at[g, 3 + k], x_r.at[n, g, 4 + c], dev(at(dx=2, core=k))))
             for dx in (1, 3):
                 for k in (0, 1):
                     t, back = dx * 2 + k, (NX - dx) * 2 + c
@@ -132,12 +151,6 @@
             return [remote(qbuf.at[dx - 1, span],
                            pick.at[n, span, pl.ds(pl.multiple_of((dx * 2 + c) * B + MAIN, SLAB), SLAB)],
                            p_s.at[g, dx - 1], p_r.at[n, g, dx - 1], mate) for dx in (1, 2, 3)]
-
-        def relays(g):
-            span = span_of(g)
-            rows = pl.ds(pl.multiple_of((4 + c) * B, B), MAIN)
-            return [remote(rbuf.at[n, k, span], pick.at[n, span, rows], r_s.at[g, k],
-                           x_r.at[n, g, 4 + c], dev(at(dx=dx, core=k))) for k, dx in ((0, 1), (1, 3))]
 
         def choose(blocks, table, pos, rows):
             total = None
@@ -165,11 +178,6 @@
                     rows = pl.ds(pl.multiple_of((dx * 2 + c) * B + MAIN, SLAB), SLAB)
                     pick[n, pos, rows, :] = choose(blocks, 8 + dx - 1, pos, SLAB)
             for copy in slab_sends(g):
-                copy.start()
-
-        def relay(g):
-            for k, copy in enumerate(relays(g)):
-                arrives(rbuf.at[n, k, span_of(g)], r_r.at[n, g, k])()
                 copy.start()
 
         def apply(g):
@@ -200,16 +208,18 @@
                                  preferred_element_type=jnp.float32)
                 items[n, 0, k] = solved.astype(jnp.bfloat16)
 
-        goes_up = [y <= 3, y <= 2]
-        goes_down = [(y == 0) | (y >= 6), (y == 0) | (y >= 5)]
+        for k in range(NB):
+            for i in (2 * k, 2 * k + 1):
+                pl.when(y != 0)(arrives(piece(i), bc_r.at[n, i]))
+                for way in (0, 1):
+                    goes, copy = bcast(i, way)
+                    pl.when(goes)(copy.start)
+            ring(0, 1, k, 1).start()
+            ring(0, 7, k, -1).start()
         for i in range(8):
-            piece = items.at[n, 0, i // 2, pl.ds((i % 2) * (B // 2), B // 2)]
-            pl.when(y != 0)(arrives(piece, bc_r.at[n, i]))
-            pl.when(goes_up[i // 4])(bcast(i, up, 0).start)
-            pl.when(goes_down[i // 4])(bcast(i, down, 1).start)
-            if i % 2 == 1:
-                ring(0, 1, i // 2, 1).start()
-                ring(0, 7, i // 2, -1).start()
+            for way in (2, 3):
+                goes, copy = bcast(i, way)
+                pl.when(goes)(copy.start)
         for copy in slab_start():
             copy.start()
 
@@ -269,45 +279,25 @@
             slab_ring(0, 7, k, -1).start()
         hop(ring, 4, 2)
         pass_on(2)
-        relay(0)
+        slab_pass(0)
         hop(slab_ring, 2, 1)
-        slab_pass(0)
         hop(ring, 4, 3)
         pass_on(3)
-        relay(1)
+        slab_pass(1)
         hop(slab_ring, 2, 2)
-        slab_pass(1)
-
-        @pl.when(first)
-        def _():
-            loads[3].wait()
-
-            def place(s, carry):
-                code = enc[s]
-                row = jnp.where(code < 0, -1, (code >> 2) & 3)
-                block = zf[jnp.maximum(code, 0) >> 4].astype(jnp.bfloat16)
-                pos, col = lax.div(s, 8), lax.rem(s, 8)
-                for r in range(NB):
-                    keep = jnp.where(row == r, 1.0, 0.0).astype(jnp.bfloat16)
-                    w[pos, pl.ds(r * B, B), pl.ds(pl.multiple_of(col * B, B), B)] = block * keep
-                return carry
-
-            lax.fori_loop(0, 64, place, 0)
 
         last(ring, 4)
         pass_on(4)
-        relay(2)
+        slab_pass(2)
         apply(0)
         hop(slab_ring, 2, 3)
-        slab_pass(2)
-        relay(3)
+        slab_pass(3)
         apply(1)
+        apply(2)
         last(slab_ring, 2)
-        slab_pass(3)
         slab_pass(4)
-        relay(4)
-        for g in range(2, 5):
-            apply(g)
+        apply(3)
+        apply(4)
 
         pl.when(y != NY - 1)(move.wait_recv)
 
@@ -320,8 +310,9 @@
             part[n + 1] = acc[...]
 
         for i in range(8):
-            pl.when(goes_up[i // 4])(bcast(i, up, 0).wait_send)
-            pl.when(goes_down[i // 4])(bcast(i, down, 1).wait_send)
+            for way in range(4):
+                goes, copy = bcast(i, way)
+                pl.when(goes)(copy.wait_send)
         for make, pieces in ((ring, 4), (slab_ring, 2)):
             for k in range(pieces):
                 for h in range(3):
@@ -331,7 +322,7 @@
         for copy in slab_start():
             copy.wait_send()
         for g in range(5):
-            for copy in sends(g) + relays(g) + slab_sends(g):
+            for copy in sends(g) + slab_sends(g):
                 copy.wait_send()
         pl.when(y != 0)(move.wait_send)
         return carry
@@ -377,7 +368,6 @@
             pltpu.VMEM((6, NZ, MAIN, EXC), jnp.bfloat16),
             pltpu.VMEM((NZ, B, EXC), jnp.bfloat16),
             pltpu.VMEM((NX - 1, NZ, SLAB, EXC), jnp.bfloat16),
-            pltpu.VMEM((STEPS, 2, NZ, MAIN, EXC), jnp.bfloat16),
             pltpu.VMEM((STEPS + 1, OWN, EXC), jnp.float32),
             pltpu.VMEM((STEPS, OWN, EXC), jnp.float32),
             pltpu.VMEM((OWN, EXC), jnp.float32),
@@ -385,9 +375,9 @@
             pltpu.VMEM((8, NZ * NB, EXC), jnp.float32),
             pltpu.VMEM((NX - 1, NZ * NB, EXC), jnp.float32),
             pltpu.VMEM((14, NZ * NB, 16, EXC), jnp.bfloat16),
-            dma((4,)), dma((STEPS, 8)), dma((STEPS, NZ, 4)), dma((STEPS, NZ, 3)), dma((STEPS, 5, 8)), dma((STEPS, 5, 2)),
+            dma((4,)), dma((STEPS, 8)), dma((STEPS, NZ, 4)), dma((STEPS, NZ, 3)), dma((STEPS, 5, 8)),
             dma((STEPS, 5, 3)), dma((STEPS,)), dma((11,)),
-            dma((2, 8)), dma((NZ, 4)), dma((NZ, 3)), dma((5, 7)), dma((5, 2)), dma((5, 3)), dma, dma((10,)),
+            dma((4, 8)), dma((NZ, 4)), dma((NZ, 3)), dma((5, 7)), dma((5, 3)), dma, dma((10,)),
         ],
         compiler_params=pltpu.CompilerParams(collective_id=0, has_side_effects=True,
                                              vmem_limit_bytes=48 * 1024 * 1024),

time: 145 us -> 136 us (0.938)
  the two profiles are of different devices: /device:TPU:32 before, /device:TPU:41 now
where the time goes in v5:
time: 136 us
  Pallas kernels  131 us (96%)
  other arithmetic  2.32 us (2%)
  local copies, waits for them, and re-layouts  1.5 us (1%)
    pallas_call x1, Pallas kernels, body(): pl.pallas_call(kernel, out_shape=(jax.ShapeDtypeStruct((STEPS, OWN, EXC),...  131 us

profile of v5, /device:TPU:41, one launch (start us, length us, event | category | flops | bytes accessed | tf_op | source)
XLA Modules:
  0.0 135.9 jit_solution(17849666566824292632)
XLA Ops:
  0.7 0.9 select_reduce_fusion
  1.5 0.7 fusion.3
  2.2 0.7 broadcast_compare_fusion
  2.9 0.1 select_reduce_fusion.1.enc
  3.0 131.4 %shard_map.86 = (bf16[4,512,128]{2,1,0:T(8,128)(2,1)S(1)}, f32[1,512,128]{2,1,0:T(8,128)S(1)}) custom-call(s32[64]{0:T(128)S(1)} %select_reduce_fusion.1.enc, bf16[4,512,128]{2,1,0:T(8,128)(2,1)} %inc_hbm.1, f32[1,512,128]{2,1,0:T(8,128)} %pend.1, f32[4,128,128]{2,1,0:T(8,128)} %sinv_hbm.1, f32[1,1,56,128,128]{4,3,2,1,0:T(8,128)} %zmat.1), custom_call_target="tpu_custom_call" | custom-call | tf_op jit(solution)/shard_map/pallas_call | solution.py:354
  134.4 0.8 copy.11
  135.2 0.7 copy.12

commit v6 on v5

--- a/solution.py
+++ b/solution.py
@@ -63,20 +63,8 @@
         return carry
 
     lax.fori_loop(0, 64, ask, 0)
-    for load in loads:
+    for load in loads[:3]:
         load.wait()
-
-    def place(s, carry):
-        code = enc[s]
-        row = jnp.where(code < 0, -1, (code >> 2) & 3)
-        block = zf[jnp.maximum(code, 0) >> 4].astype(jnp.bfloat16)
-        pos, col = lax.div(s, 8), lax.rem(s, 8)
-        for r in range(NB):
-            keep = jnp.where(row == r, 1.0, 0.0).astype(jnp.bfloat16)
-            w[pos, pl.ds(r * B, B), pl.ds(pl.multiple_of(col * B, B), B)] = block * keep
-        return carry
-
-    lax.fori_loop(0, 64, place, 0)
     pl.semaphore_wait(barrier, len(peers))
 
     def remote(src, dst, ssem, rsem, where):
@@ -277,6 +265,22 @@
         for k in range(2):
             slab_ring(0, 1, k, 1).start()
             slab_ring(0, 7, k, -1).start()
+        @pl.when(first)
+        def _():
+            loads[3].wait()
+
+            def place(s, carry):
+                code = enc[s]
+                row = jnp.where(code < 0, -1, (code >> 2) & 3)
+                block = zf[jnp.maximum(code, 0) >> 4].astype(jnp.bfloat16)
+                pos, col = lax.div(s, 8), lax.rem(s, 8)
+                for r in range(NB):
+                    keep = jnp.where(row == r, 1.0, 0.0).astype(jnp.bfloat16)
+                    w[pos, pl.ds(r * B, B), pl.ds(pl.multiple_of(col * B, B), B)] = block * keep
+                return carry
+
+            lax.fori_loop(0, 64, place, 0)
+
         hop(ring, 4, 2)
         pass_on(2)
         slab_pass(0)
@@ -338,16 +342,16 @@
     x, z = (p // 2) % NX, p // (2 * NX)
     row = block_rows[0, 0]
     source = block_sources[0, 0]
-    live = source >= 0
-    storage = jnp.sum(jnp.where(source[:, None] == jnp.arange(SRC)[None, :], owner_map[None, :], 0), axis=1)
+    storage = jnp.max(jnp.where(source[:, None] == jnp.arange(SRC)[None, :], owner_map[None, :], -1), axis=1)
     owner, local = storage // NB, storage % NB
     d = (z - owner // (2 * NX)) % NZ
     pos = jnp.where(d == 0, 0, jnp.where(d <= 3, 2 * d - 1, jnp.where(d == 4, 7, 2 * (NZ - d))))
     column = ((owner // 2) % NX - x) % NX * 2 + owner % 2
     slot = pos * 8 + column
-    code = jnp.arange(LIST, dtype=jnp.int32) * 16 + row * 4 + local
-    hit = (slot[None, :] == jnp.arange(64)[:, None]) & live[None, :]
+    code = jnp.where(storage < 0, -1, jnp.arange(LIST, dtype=jnp.int32) * 16 + row * 4 + local)
+    hit = slot[None, :] == jnp.arange(64)[:, None]
     enc = jnp.max(jnp.where(hit, code[None, :], -1), axis=1).astype(jnp.int32)
+
     vmem = pl.BlockSpec(memory_space=pltpu.VMEM)
     hbm = pl.BlockSpec(memory_space=pltpu.HBM)
     dma = pltpu.SemaphoreType.DMA

time: 136 us -> 134 us (0.985)
  no operation moved by 1% of the time
where the time goes in v6:
time: 134 us
  Pallas kernels  130 us (97%)
  other arithmetic  1.66 us (1%)
  local copies, waits for them, and re-layouts  1.5 us (1%)
    pallas_call x1, Pallas kernels, body(): pl.pallas_call(kernel, out_shape=(jax.ShapeDtypeStruct((STEPS, OWN, EXC),...  130 us

profile of v6, /device:TPU:41, one launch (start us, length us, event | category | flops | bytes accessed | tf_op | source)
XLA Modules:
  0.0 134.2 jit_solution(8975853787404718212)
XLA Ops:
  0.7 0.9 select_reduce_fusion
  1.5 0.7 fusion.3
  2.2 0.1 select_reduce_fusion.1.enc
  2.3 130.4 %shard_map.86 = (bf16[4,512,128]{2,1,0:T(8,128)(2,1)S(1)}, f32[1,512,128]{2,1,0:T(8,128)S(1)}) custom-call(s32[64]{0:T(128)S(1)} %select_reduce_fusion.1.enc, bf16[4,512,128]{2,1,0:T(8,128)(2,1)} %inc_hbm.1, f32[1,512,128]{2,1,0:T(8,128)} %pend.1, f32[4,128,128]{2,1,0:T(8,128)} %sinv_hbm.1, f32[1,1,56,128,128]{4,3,2,1,0:T(8,128)} %zmat.1), custom_call_target="tpu_custom_call" | custom-call | tf_op jit(solution)/shard_map/pallas_call | solution.py:358
  132.7 0.8 copy.11
  133.5 0.7 copy.12

commit v7 on v6

--- a/solution.py
+++ b/solution.py
@@ -63,6 +63,16 @@
         return carry
 
     lax.fori_loop(0, 64, ask, 0)
+
+    def line(rows):
+        return jnp.broadcast_to(rows, (16, EXC)).astype(jnp.bfloat16)
+
+    def spread_own(i, carry):
+        for r in range(NB * NZ):
+            onehot[8 + i, r] = line(want[i * 2 + 2 + c, pl.ds(r, 1), :])
+        return carry
+
+    lax.fori_loop(0, 3, spread_own, 0)
     for load in loads[:3]:
         load.wait()
     pl.semaphore_wait(barrier, len(peers))
@@ -222,9 +232,6 @@
             for dx in (1, 2, 3):
                 arrives(wanted2.at[dx - 1], q_r.at[7 + dx])()
 
-            def line(rows):
-                return jnp.broadcast_to(rows, (16, EXC)).astype(jnp.bfloat16)
-
             def spread(t, carry):
                 for r in range(NB * NZ):
                     onehot[t, r] = line(wanted[t, pl.ds(r, 1), :])
@@ -232,7 +239,6 @@
 
             def spread_slabs(i, carry):
                 for r in range(NB * NZ):
-                    onehot[8 + i, r] = line(want[i * 2 + 2 + c, pl.ds(r, 1), :])
                     onehot[11 + i, r] = line(wanted2[i, pl.ds(r, 1), :])
                 return carry
 

time: 134 us -> 134 us (level)
  no operation moved by 1% of the time
where the time goes in v7:
time: 134 us
  Pallas kernels  130 us (97%)
  other arithmetic  1.66 us (1%)
  local copies, waits for them, and re-layouts  1.5 us (1%)
    pallas_call x1, Pallas kernels, body(): pl.pallas_call(kernel, out_shape=(jax.ShapeDtypeStruct((STEPS, OWN, EXC),...  130 us

profile of v7, /device:TPU:41, one launch (start us, length us, event | category | flops | bytes accessed | tf_op | source)
XLA Modules:
  0.0 134.2 jit_solution(14879368454912921580)
XLA Ops:
  0.7 0.9 select_reduce_fusion
  1.5 0.7 fusion.3
  2.2 0.1 select_reduce_fusion.1.enc
  2.3 130.4 %shard_map.86 = (bf16[4,512,128]{2,1,0:T(8,128)(2,1)S(1)}, f32[1,512,128]{2,1,0:T(8,128)S(1)}) custom-call(s32[64]{0:T(128)S(1)} %select_reduce_fusion.1.enc, bf16[4,512,128]{2,1,0:T(8,128)(2,1)} %inc_hbm.1, f32[1,512,128]{2,1,0:T(8,128)} %pend.1, f32[4,128,128]{2,1,0:T(8,128)} %sinv_hbm.1, f32[1,1,56,128,128]{4,3,2,1,0:T(8,128)} %zmat.1), custom_call_target="tpu_custom_call" | custom-call | tf_op jit(solution)/shard_map/pallas_call | solution.py:364
  132.7 0.8 copy.11
  133.5 0.7 copy.12
